TPU v7x, 32 devices: a whole 2x2x4 slice. The times are simulated.
32 devices in a mesh: frame: 4 (over z), pipe: 4 (over x, core), dp: 2 (over y).
Axes of the slice: x: 2, y: 2, z: 4, core: 2. Of those that a mesh axis runs over, the one named last changes fastest.
Arguments:
- acts: bfloat16 [4, 2, 32, 4, 1280], P('pipe', 'dp', 'frame'), may hold values from -18 to 18
- cotangent: bfloat16 [4, 2, 32, 4, 1280], P('pipe', 'dp', 'frame'), may hold values from -6 to 6
- w_query: bfloat16 [4, 1280, 768], P('pipe'), may hold values from -0.15625 to 0.15625
- w_key: bfloat16 [4, 1280, 768], P('pipe'), may hold values from -0.15625 to 0.15625
- w_value: bfloat16 [4, 1280, 768], P('pipe'), may hold values from -0.15625 to 0.15625
- w_out: bfloat16 [4, 1280, 768], P('pipe'), may hold values from -0.21875 to 0.21875
Outputs:
- sent_grad: bfloat16 [4, 2, 32, 4, 1280], P('pipe', 'dp', 'frame')
- grad_value: float32 [4, 1280, 768], P('pipe', None, ('frame', 'dp'))
All inputs are finite; a program needn't handle non-finite values.
Results may differ from a plain program's by a relative error of at most 0.017.
The roundings to bfloat16 on the way count: a program that leaves them out, or rounds other values in their place, can miss the bound.
Values may be sent and summed in bfloat16 or wider, within the bound.
No kernel may reach another device: no remote copies, remote signals or barrier semaphores. Data moves between devices by JAX's collectives and lax.ppermute only.
A program may use at most 64 MiB of HBM per device.

v0:
```python
import jax
import jax.numpy as jnp
from jax import lax
from jax.sharding import PartitionSpec as P

HEADS = 12
HEAD_DIM = 64


score_scale = 0.125


def shifted(shard, axis, by):
    count = lax.axis_size(axis)
    pairs = [(i, i + by) for i in range(count) if 0 <= i + by < count]
    return lax.ppermute(shard, axis, pairs)


def attend_back(inputs, projected, w_query, w_key, w_value):
    frames = inputs.shape[0]
    places = inputs.shape[1]

    def project_heads(weight):
        result = jnp.dot(inputs, weight, preferred_element_type=jnp.float32).astype(jnp.bfloat16)
        return result.reshape(frames, places, HEADS, HEAD_DIM)

    queries = project_heads(w_query)
    key_rows = project_heads(w_key)
    values = project_heads(w_value)
    scores = (
        jnp.einsum("iphd,jphd->phij", queries, key_rows, preferred_element_type=jnp.float32)
        * score_scale
    )
    probability = jax.nn.softmax(scores, axis=-1)
    prob_short = probability.astype(jnp.bfloat16)
    proj_heads = projected.reshape(frames, places, HEADS, HEAD_DIM)
    grad_prob = jnp.einsum(
        "iphd,jphd->phij", proj_heads, values, preferred_element_type=jnp.float32
    )
    value_grad = jnp.einsum(
        "phij,iphd->jphd", prob_short, proj_heads, preferred_element_type=jnp.float32
    ).astype(jnp.bfloat16)
    score_grad = probability * (
        grad_prob - jnp.sum(grad_prob * probability, axis=-1, keepdims=True)
    )
    score_short = score_grad.astype(jnp.bfloat16)
    query_grad = (
        jnp.einsum("phij,jphd->iphd", score_short, key_rows, preferred_element_type=jnp.float32)
        * score_scale
    ).astype(jnp.bfloat16)
    key_grad = (
        jnp.einsum("phij,iphd->jphd", score_short, queries, preferred_element_type=jnp.float32)
        * score_scale
    ).astype(jnp.bfloat16)
    inner = HEADS * HEAD_DIM
    query_grad = query_grad.reshape(frames, places, inner)
    key_grad = key_grad.reshape(frames, places, inner)
    value_grad = value_grad.reshape(frames, places, inner)
    branch = jnp.einsum("fpj,cj->fpc", query_grad, w_query, preferred_element_type=jnp.float32)
    branch = branch + jnp.einsum("fpj,cj->fpc", key_grad, w_key, preferred_element_type=jnp.float32)
    branch = branch + jnp.einsum(
        "fpj,cj->fpc", value_grad, w_value, preferred_element_type=jnp.float32
    )
    branch = branch.astype(jnp.bfloat16)
    weight_grad = jnp.einsum("fpc,fpj->cj", inputs, value_grad, preferred_element_type=jnp.float32)
    return (branch, weight_grad)


def body(acts, cotangent, w_query, w_key, w_value, w_out):
    inputs = acts[0, 0]
    upstream = cotangent[0, 0]
    query_weight = w_query[0]
    key_weight = w_key[0]
    value_weight = w_value[0]
    out_weight = w_out[0]
    row_inputs, row_upstream = (
        lax.all_to_all(inputs, "frame", split_axis=1, concat_axis=0, tiled=True),
        lax.all_to_all(upstream, "frame", split_axis=1, concat_axis=0, tiled=True),
    )
    projected = jnp.dot(row_upstream, out_weight, preferred_element_type=jnp.float32).astype(
        jnp.bfloat16
    )
    branch, value_grad = attend_back(row_inputs, projected, query_weight, key_weight, value_weight)
    row_result = (row_upstream.astype(jnp.float32) + branch.astype(jnp.float32)).astype(
        jnp.bfloat16
    )
    frame_result = lax.all_to_all(row_result, "frame", split_axis=0, concat_axis=1, tiled=True)
    sent_grad = shifted(frame_result[None, None], "pipe", -1)
    value_middle = lax.psum_scatter(
        value_grad.astype(jnp.bfloat16), "frame", scatter_dimension=1, tiled=True
    )
    value_part = lax.psum_scatter(value_middle, "dp", scatter_dimension=1, tiled=True).astype(
        jnp.float32
    )
    return (sent_grad, value_part[None])


def solution(mesh):
    return jax.shard_map(
        body,
        mesh=mesh,
        in_specs=(
            P("pipe", "dp", "frame", None, None),
            P("pipe", "dp", "frame", None, None),
            P("pipe", None, None),
            P("pipe", None, None),
            P("pipe", None, None),
            P("pipe", None, None),
        ),
        out_specs=(P("pipe", "dp", "frame", None, None), P("pipe", None, ("frame", "dp"))),
        check_vma=False,
    )
```

profile of v0, /device:TPU:1, one launch (start us, length us, event | category | flops | bytes accessed | tf_op | source)
XLA Modules:
  0.0 102.3 jit_solution(5683003131072736057)
XLA Ops:
  7.2 1.7 %copy.98 = bf16[1,1,8,4,1280]{4,2,3,1,0:T(8,128)(2,1)} copy(bf16[1,1,8,4,1280]{4,3,2,1,0:T(4,128)(2,1)} %param.6) | data formatting | bytes 163840 | tf_op args[0]
  8.9 5.4 %all-to-all-start.1 = ((bf16[8,4,1280]{2,0,1:T(8,128)(2,1)}), bf16[8,4,1280]{2,0,1:T(8,128)(2,1)S(1)}, u32[]{:S(2)}, u32[]{:S(2)}) async-start(bf16[8,4,1280]{2,0,1:T(8,128)(2,1)} %bitcast.89), calls=%async_computation.1 | async-start | bytes 163840 | tf_op jit(solution)/shard_map/all_to_all | solution.py:77
  14.3 1.5 %copy.99 = bf16[1,1,8,4,1280]{4,2,3,1,0:T(8,128)(2,1)} copy(bf16[1,1,8,4,1280]{4,3,2,1,0:T(4,128)(2,1)} %param.7) | data formatting | bytes 163840 | tf_op args[1]
  15.8 3.1 %all-to-all-done.1 = bf16[8,4,1280]{2,0,1:T(8,128)(2,1)S(1)} async-done(((bf16[8,4,1280]{2,0,1:T(8,128)(2,1)}), bf16[8,4,1280]{2,0,1:T(8,128)(2,1)S(1)}, u32[]{:S(2)}, u32[]{:S(2)}) %all-to-all-start.1) | async-done | bytes 81952 | tf_op jit(solution)/shard_map/all_to_all | solution.py:77
  18.9 3.3 %all-to-all-start = ((bf16[8,4,1280]{2,0,1:T(8,128)(2,1)}), bf16[8,4,1280]{2,0,1:T(8,128)(2,1)S(1)}, u32[]{:S(2)}, u32[]{:S(2)}) async-start(bf16[8,4,1280]{2,0,1:T(8,128)(2,1)} %bitcast.90), calls=%async_computation | async-start | bytes 163840 | tf_op jit(solution)/shard_map/all_to_all | solution.py:78
  22.3 0.5 fusion.29
  22.7 1.1 %copy-done.1 = bf16[1,1280,768]{2,1,0:T(8,128)(2,1)S(1)} copy-done((bf16[1,1280,768]{2,1,0:T(8,128)(2,1)S(1)}, bf16[1,1280,768]{2,1,0:T(8,128)(2,1)}, u32[]{:S(2)}) %copy-start.1) | copy-done | bytes 1966104
  23.8 0.5 fusion.26
  24.3 0.1 reshape.127
  24.6 2.2 %all-to-all-done = bf16[8,4,1280]{2,0,1:T(8,128)(2,1)S(1)} async-done(((bf16[8,4,1280]{2,0,1:T(8,128)(2,1)}), bf16[8,4,1280]{2,0,1:T(8,128)(2,1)S(1)}, u32[]{:S(2)}, u32[]{:S(2)}) %all-to-all-start) | async-done | bytes 81952 | tf_op jit(solution)/shard_map/all_to_all | solution.py:78
  26.8 2.0 %fusion.32 = bf16[32,768]{1,0:T(8,128)(2,1)S(1)} fusion(bf16[1,1280,768]{2,1,0:T(8,128)(2,1)} %param.11, bf16[8,4,1280]{2,0,1:T(8,128)(2,1)S(1)} %all-to-all-done), kind=kOutput, calls=%fused_computation.35 | convolution fusion | flops 62939136 | bytes 2097152 | tf_op jit(solution)/shard_map/dot_general | solution.py:80
  28.8 0.1 reshape.129
  29.0 0.2 fusion.62
  29.2 0.2 fusion.23
  29.5 2.0 %fusion.1 = bf16[1280,768]{0,1:T(8,128)(2,1)} fusion(bf16[32,768]{1,0:T(8,128)(2,1)S(1)} %reshape.133, bf16[8,4,1280]{2,0,1:T(8,128)(2,1)S(1)} %all-to-all-done.1), kind=kOutput, calls=%fused_computation.2 | convolution fusion | flops 63897600 | bytes 2097152 | tf_op jit(solution)/shard_map/fpc,fpj->cj/dot_general | solution.py:65
  31.6 2.0 %fusion.35 = bf16[32,768]{1,0:T(8,128)(2,1)S(1)} fusion(bf16[1,1280,768]{2,1,0:T(8,128)(2,1)} %param.10, bf16[8,4,1280]{2,0,1:T(8,128)(2,1)S(1)} %all-to-all-done.1), kind=kOutput, calls=%fused_computation.36 | convolution fusion | flops 62939136 | bytes 2097152 | tf_op jit(solution)/shard_map/dot_general | solution.py:24
  33.6 0.1 reshape.130
  33.8 0.2 multiply_reduce_fusion
  34.0 0.2 fusion.25
  34.4 0.2 fusion.24
  34.8 39.4 %reduce-scatter.3.cloned.1.call-done = bf16[1280,192]{0,1:T(8,128)(2,1)} async-done(((bf16[1280,768]{0,1:T(8,128)(2,1)}), bf16[1280,192]{0,1:T(8,128)(2,1)}) %reduce-scatter.3.cloned.1.call-update) | async-done | bytes 491536 | tf_op jit(solution)/shard_map/reduce_scatter | solution.py:89
  74.2 0.7 fusion.12
  74.9 0.8 copy-done.2
  75.7 0.7 convolution_add_fusion.1
  76.4 0.7 fusion.6
  77.1 0.5 broadcast.23
  77.7 0.7 reduce.6
  78.4 7.6 %all_to_all.48 = bf16[4,2,5120]{2,1,0:T(2,128)(2,1)S(1)} all-to-all(bf16[4,2,5120]{2,1,0:T(2,128)(2,1)S(1)} %reshape.135), channel_id=1, replica_groups=mesh['frame'=4,'pipe'=4,'dp'=2] {'frame'}, dimensions={0} | all-to-all | bytes 163840 | tf_op jit(solution)/shard_map/all_to_all | solution.py:87
  86.1 3.9 %collective-permute-start = (bf16[1,1,8,4,1280]{4,2,3,1,0:T(8,128)(2,1)S(1)}, bf16[1,1,8,4,1280]{4,2,3,1,0:T(8,128)(2,1)S(1)}, u32[]{:S(2)}, u32[]{:S(2)}) collective-permute-start(bf16[1,1,8,4,1280]{4,2,3,1,0:T(8,128)(2,1)S(1)} %bitcast.91), channel_id=1, source_target_pairs={{2,0},{4,2},{6,4},{3,1},{5,3},{7,5},{10,8},{12,10},{14,12},{11,9},... | collective-permute-start | bytes 245768 | tf_op jit(solution)/shard_map/ppermute | solution.py:16
  90.0 3.0 %collective-permute-done = bf16[1,1,8,4,1280]{4,2,3,1,0:T(8,128)(2,1)S(1)} collective-permute-done((bf16[1,1,8,4,1280]{4,2,3,1,0:T(8,128)(2,1)S(1)}, bf16[1,1,8,4,1280]{4,2,3,1,0:T(8,128)(2,1)S(1)}, u32[]{:S(2)}, u32[]{:S(2)}) %collective-permute-start) | collective-permute-done | bytes 81952 | tf_op jit(solution)/shard_map/ppermute | solution.py:16
  93.0 0.7 copy.61
  93.7 1.8 %bitcast_convert_fusion = f32[1,1280,96]{1,2,0:T(8,128)} fusion(bf16[1280,96]{0,1:T(8,128)(2,1)} %reduce-scatter.5.cloned.1.call-done), kind=kLoop, calls=%fused_computation.37 | loop fusion | flops 122880 | bytes 737280 | tf_op jit(solution)/shard_map/broadcast_in_dim | solution.py:95
  (22 shorter events, 1.0 us)
Async XLA Ops:
  7.2 15.1 %copy-start = (bf16[1,1280,768]{2,1,0:T(8,128)(2,1)S(1)}, bf16[1,1280,768]{2,1,0:T(8,128)(2,1)}, u32[]{:S(2)}) copy-start(bf16[1,1280,768]{2,1,0:T(8,128)(2,1)} %param.8) | copy-start | bytes 5898244
  8.9 10.0 %all-to-all-start.1 = ((bf16[8,4,1280]{2,0,1:T(8,128)(2,1)}), bf16[8,4,1280]{2,0,1:T(8,128)(2,1)S(1)}, u32[]{:S(2)}, u32[]{:S(2)}) async-start(bf16[8,4,1280]{2,0,1:T(8,128)(2,1)} %bitcast.89), calls=%async_computation.1 | async-start | bytes 163840 | tf_op jit(solution)/shard_map/all_to_all | solution.py:77
  18.9 7.9 %all-to-all-start = ((bf16[8,4,1280]{2,0,1:T(8,128)(2,1)}), bf16[8,4,1280]{2,0,1:T(8,128)(2,1)S(1)}, u32[]{:S(2)}, u32[]{:S(2)}) async-start(bf16[8,4,1280]{2,0,1:T(8,128)(2,1)} %bitcast.90), calls=%async_computation | async-start | bytes 163840 | tf_op jit(solution)/shard_map/all_to_all | solution.py:78
  22.2 51.9 %reduce-scatter.3.cloned.1.call-start = ((), (), s32[]{:S(2)}) async-start(), calls=%async_computation.5 | async-start | bytes 2457600 | tf_op jit(solution)/shard_map/reduce_scatter | solution.py:89
  22.3 1.5 %copy-start.1 = (bf16[1,1280,768]{2,1,0:T(8,128)(2,1)S(1)}, bf16[1,1280,768]{2,1,0:T(8,128)(2,1)}, u32[]{:S(2)}) copy-start(bf16[1,1280,768]{2,1,0:T(8,128)(2,1)} %param.9) | copy-start | bytes 5898244
  31.5 62.2 %reduce-scatter.5.cloned.1.call-start = ((), (), s32[]{:S(2)}) async-start(), calls=%async_computation.6 | async-start | bytes 737280 | tf_op jit(solution)/shard_map/reduce_scatter | solution.py:92
  74.2 1.5 %copy-start.2 = (bf16[1,1280,768]{2,1,0:T(8,128)(2,1)S(1)}, bf16[1,1280,768]{2,1,0:T(8,128)(2,1)}, u32[]{:S(2)}) copy-start(bf16[1,1280,768]{2,1,0:T(8,128)(2,1)} %param.9) | copy-start | bytes 5898244
  74.2 2.2 %copy-start.3 = (bf16[1,1280,768]{2,1,0:T(8,128)(2,1)S(1)}, bf16[1,1280,768]{2,1,0:T(8,128)(2,1)}, u32[]{:S(2)}) copy-start(bf16[1,1280,768]{2,1,0:T(8,128)(2,1)} %param.10) | copy-start | bytes 5898244
  86.1 6.9 %collective-permute-start = (bf16[1,1,8,4,1280]{4,2,3,1,0:T(8,128)(2,1)S(1)}, bf16[1,1,8,4,1280]{4,2,3,1,0:T(8,128)(2,1)S(1)}, u32[]{:S(2)}, u32[]{:S(2)}) collective-permute-start(bf16[1,1,8,4,1280]{4,2,3,1,0:T(8,128)(2,1)S(1)} %bitcast.91), channel_id=1, source_target_pairs={{2,0},{4,2},{6,4},{3,1},{5,3},{7,5},{10,8},{12,10},{14,12},{11,9},... | collective-permute-start | bytes 245768 | tf_op jit(solution)/shard_map/ppermute | solution.py:16
Sparse Core Ops, SparseCore 0:
  31.7 42.4 reduce-scatter.2
  76.4 13.5 reduce-scatter.4
where the time goes:
time: 103 us; the launch traced here: 102 us
  waiting for transfers between devices  47.8 us (46%)
  between operations  14.2 us (14%)
  starting transfers between devices  12.7 us (12%)
  matrix products  9.96 us (10%)
  blocking collectives  7.64 us (7%)
  local copies, waits for them, and re-layouts  7.55 us (7%)
  other arithmetic  2.47 us (2%)
    reduce_scatter x1, waiting for transfers between devices, body(): lax.psum_scatter(value_grad.astype(jnp.bfloat16), 'frame', scatter_dimens...  39.4 us
    all_to_all x1, blocking collectives, body(): lax.all_to_all(row_result, 'frame', split_axis=0, concat_axis=1, tiled=True)  7.64 us
    unnamed x14, local copies, waits for them, and re-layouts  5.91 us
    all_to_all x1, starting transfers between devices, body(): lax.all_to_all(inputs, 'frame', split_axis=1, concat_axis=0, tiled=True)  5.41 us
    ppermute x1, starting transfers between devices, shifted(): return lax.ppermute(shard, axis, pairs)  3.88 us
    all_to_all x1, starting transfers between devices, body(): lax.all_to_all(upstream, 'frame', split_axis=1, concat_axis=0, tiled=True)  3.3 us
    all_to_all x1, waiting for transfers between devices, body(): lax.all_to_all(inputs, 'frame', split_axis=1, concat_axis=0, tiled=True)  3.11 us
    ppermute x1, waiting for transfers between devices, shifted(): return lax.ppermute(shard, axis, pairs)  3.04 us
  transfers between devices with their start and end apart: 5, of which 4 were waited for; matrix products, arithmetic and copies ran while one was open for 10% of the time, Pallas kernels for 0%

commit v1 on v0

--- a/solution.py
+++ b/solution.py
@@ -1,7 +1,12 @@
+import functools
+
 import jax
 import jax.numpy as jnp
 from jax import lax
+from jax.experimental import pallas as pl
+from jax.experimental.pallas import tpu as pltpu
 from jax.sharding import PartitionSpec as P
+
 
 HEADS = 12
 HEAD_DIM = 64
@@ -14,6 +19,11 @@
     count = lax.axis_size(axis)
     pairs = [(i, i + by) for i in range(count) if 0 <= i + by < count]
     return lax.ppermute(shard, axis, pairs)
+
+
+def rotated(shard, axis, by):
+    count = lax.axis_size(axis)
+    return lax.ppermute(shard, axis, [(i, (i + by) % count) for i in range(count)])
 
 
 def attend_back(inputs, projected, w_query, w_key, w_value):
@@ -66,21 +76,17 @@
     return (branch, weight_grad)
 
 
-def body(acts, cotangent, w_query, w_key, w_value, w_out):
+def general_body(acts, cotangent, w_query, w_key, w_value, w_out):
     inputs = acts[0, 0]
     upstream = cotangent[0, 0]
-    query_weight = w_query[0]
-    key_weight = w_key[0]
-    value_weight = w_value[0]
-    out_weight = w_out[0]
     row_inputs, row_upstream = (
         lax.all_to_all(inputs, "frame", split_axis=1, concat_axis=0, tiled=True),
         lax.all_to_all(upstream, "frame", split_axis=1, concat_axis=0, tiled=True),
     )
-    projected = jnp.dot(row_upstream, out_weight, preferred_element_type=jnp.float32).astype(
+    projected = jnp.dot(row_upstream, w_out[0], preferred_element_type=jnp.float32).astype(
         jnp.bfloat16
     )
-    branch, value_grad = attend_back(row_inputs, projected, query_weight, key_weight, value_weight)
+    branch, value_grad = attend_back(row_inputs, projected, w_query[0], w_key[0], w_value[0])
     row_result = (row_upstream.astype(jnp.float32) + branch.astype(jnp.float32)).astype(
         jnp.bfloat16
     )
@@ -95,18 +101,229 @@
     return (sent_grad, value_part[None])
 
 
+def flat_rows(ref):
+    block = ref[...]
+    frames, places, channels = block.shape
+    flat = block.astype(jnp.float32).reshape(frames * places, channels)
+    return flat.astype(jnp.bfloat16)
+
+
+def dot_nn(a, b):
+    return jnp.dot(a, b, preferred_element_type=jnp.float32)
+
+
+def dot_nt(a, b):
+    return lax.dot_general(a, b, (((1,), (1,)), ((), ())), preferred_element_type=jnp.float32)
+
+
+def dot_tn(a, b):
+    return lax.dot_general(a, b, (((0,), (0,)), ((), ())), preferred_element_type=jnp.float32)
+
+
+def project_kernel(upstream_ref, weight_ref, out_ref):
+    out_ref[...] = dot_nn(flat_rows(upstream_ref), weight_ref[...]).astype(jnp.bfloat16)
+
+
+def pair_rows(pair):
+    lane = lax.broadcasted_iota(jnp.int32, pair.shape, 1)
+    wide = pair.astype(jnp.float32)
+    first = jnp.where(lane < HEAD_DIM, wide, 0.0).astype(jnp.bfloat16)
+    second = jnp.where(lane < HEAD_DIM, 0.0, wide).astype(jnp.bfloat16)
+    return jnp.concatenate([first, second], axis=0)
+
+
+def flatten_kernel(*refs):
+    *act_refs, out_ref = refs
+    own = out_ref.shape[0] // len(act_refs)
+    for i, ref in enumerate(act_refs):
+        out_ref[i * own : (i + 1) * own, :] = flat_rows(ref)
+
+
+def forward_kernel(places, *refs):
+    row_ref, *weight_refs = refs[:4]
+    q_ref, k_ref, v_ref, prob_ref, held, sems = refs[4:]
+    copies = [
+        pltpu.make_async_copy(weight_refs[i], held.at[i], sems.at[i]) for i in range(3)
+    ]
+    for copy in copies:
+        copy.start()
+    rows = row_ref[...]
+    for i, out_ref in enumerate((q_ref, k_ref, v_ref)):
+        copies[i].wait()
+        out_ref[...] = dot_nn(rows, held[i]).astype(jnp.bfloat16)
+    count = rows.shape[0]
+    row = lax.broadcasted_iota(jnp.int32, (count, 2 * count), 0)
+    col = lax.broadcasted_iota(jnp.int32, (count, 2 * count), 1)
+    same = lax.rem(row, places) == lax.rem(col, places)
+    width = 2 * HEAD_DIM
+    for pair in range(HEADS // 2):
+        at = pl.ds(pair * width, width)
+        scores = dot_nt(k_ref[:, at], pair_rows(q_ref[:, at])) * score_scale
+        scores = jnp.where(same, scores, -jnp.inf)
+        top = jnp.max(scores, axis=0, keepdims=True)
+        raised = jnp.exp(scores - top)
+        prob_ref[pair] = raised / jnp.sum(raised, axis=0, keepdims=True)
+
+
+def value_kernel(blocks, shares, *refs):
+    prob_ref, *proj_refs = refs[: blocks + 1]
+    proj_ref, own_ref, mine_ref, send_ref, vgrad = refs[blocks + 1 :]
+    own = own_ref.shape[0]
+    for i, ref in enumerate(proj_refs):
+        proj_ref[i * own : (i + 1) * own, :] = ref[...]
+    width = 2 * HEAD_DIM
+    for pair in range(HEADS // 2):
+        at = pl.ds(pair * width, width)
+        short = prob_ref[pair].astype(jnp.bfloat16)
+        vgrad[:, at] = dot_nn(short, pair_rows(proj_ref[:, at])).astype(jnp.bfloat16)
+    own_ref[...] = vgrad[:own, :]
+    frame, member = lax.axis_index("frame"), lax.axis_index("dp")
+    inner = HEADS * HEAD_DIM
+    share = inner // shares
+    pick_row = lax.broadcasted_iota(jnp.int32, (inner, 128), 0)
+    pick_col = lax.broadcasted_iota(jnp.int32, (inner, 128), 1)
+
+    def picked(start):
+        chosen = (pick_row - pick_col == start) & (pick_col < share)
+        pick = jnp.where(chosen, 1.0, 0.0).astype(jnp.bfloat16)
+        return dot_nn(vgrad[...], pick).astype(jnp.bfloat16)
+
+    mine_ref[...] = picked((frame * lax.axis_size("dp") + member) * share)
+    send_ref[...] = picked((frame * lax.axis_size("dp") + 1 - member) * share)
+
+
+def backward_kernel(*refs):
+    prob_ref, q_ref, k_ref, v_ref, proj_ref, vgrad_ref, upstream_ref, *weight_refs = refs[:10]
+    out_ref, grads, held, sems = refs[10:]
+    copies = [
+        pltpu.make_async_copy(weight_refs[i], held.at[i], sems.at[i]) for i in (2, 0, 1)
+    ]
+    for copy in copies:
+        copy.start()
+    count = proj_ref.shape[0]
+    own = vgrad_ref.shape[0]
+    width = 2 * HEAD_DIM
+    lane = lax.broadcasted_iota(jnp.int32, (own, width), 1)
+    for pair in range(HEADS // 2):
+        at = pl.ds(pair * width, width)
+        prob = prob_ref[pair]
+        grad_prob = dot_nt(v_ref[:, at], pair_rows(proj_ref[:, at]))
+        mean = jnp.sum(grad_prob * prob, axis=0, keepdims=True)
+        score_grad = (prob * (grad_prob - mean)).astype(jnp.bfloat16)
+        key_grad = dot_nn(score_grad[:own], pair_rows(q_ref[:, at])) * score_scale
+        grads[1, :, at] = key_grad.astype(jnp.bfloat16)
+        keys = k_ref[:, at]
+        first = dot_tn(score_grad[:, :own], keys)
+        second = dot_tn(score_grad[:, count : count + own], keys)
+        query_grad = jnp.where(lane < HEAD_DIM, first, second) * score_scale
+        grads[0, :, at] = query_grad.astype(jnp.bfloat16)
+    copies[0].wait()
+    branch = dot_nt(vgrad_ref[...], held[2])
+    copies[1].wait()
+    branch = branch + dot_nt(grads[0], held[0])
+    copies[2].wait()
+    branch = branch + dot_nt(grads[1], held[1])
+    branch = branch.astype(jnp.bfloat16).astype(jnp.float32)
+    result = flat_rows(upstream_ref).astype(jnp.float32) + branch
+    out_ref[...] = result.reshape(out_ref.shape).astype(jnp.bfloat16)
+
+
+def gradient_kernel(row_ref, mine_ref, other_row_ref, other_ref, out_ref):
+    total = dot_tn(mine_ref[...], row_ref[...]) + dot_tn(other_ref[...], other_row_ref[...])
+    out_ref[...] = total[: out_ref.shape[0]]
+
+
+VMEM = pl.BlockSpec(memory_space=pltpu.VMEM)
+ANY = pl.BlockSpec(memory_space=pl.ANY)
+
+
+def call(kernel, out_shape, in_specs, scratch=(), grant=24):
+    return pl.pallas_call(
+        kernel,
+        out_shape=out_shape,
+        in_specs=in_specs,
+        out_specs=jax.tree.map(lambda _: VMEM, out_shape),
+        scratch_shapes=scratch,
+        compiler_params=pltpu.CompilerParams(vmem_limit_bytes=grant * 2**20),
+    )
+
+
+def few_rows_body(acts, cotangent, w_query, w_key, w_value, w_out):
+    inputs = acts[0, 0]
+    upstream = cotangent[0, 0]
+    frames, places, channels = inputs.shape
+    inner = w_query.shape[-1]
+    count = lax.axis_size("frame")
+    shares = count * lax.axis_size("dp")
+    own = frames * places
+    rows = count * own
+    bf16 = jnp.bfloat16
+    weights = (w_query[0], w_key[0], w_value[0])
+    shape = jax.ShapeDtypeStruct
+    turns = range(count - 1, 0, -1)
+    held = [pltpu.VMEM((3, channels, inner), bf16), pltpu.SemaphoreType.DMA((3,))]
+
+    def gathered(block):
+        received = [block]
+        for turn in turns:
+            received.append(rotated(block, "frame", turn))
+        return received
+
+    blocks = gathered(inputs)
+    projected = call(project_kernel, shape((own, inner), bf16), [VMEM, VMEM])(upstream, w_out[0])
+    all_projected = gathered(projected)
+    flat = call(flatten_kernel, shape((rows, channels), bf16), [VMEM] * count)(*blocks)
+    other_flat = rotated(flat, "dp", 1)
+    wide = shape((rows, inner), bf16)
+    queries, key_rows, values, probability = call(
+        functools.partial(forward_kernel, places),
+        (wide, wide, wide, shape((HEADS // 2, rows, 2 * rows), jnp.float32)),
+        [VMEM] + [ANY] * 3,
+        held,
+    )(flat, *weights)
+    narrow = shape((rows, 128), bf16)
+    joined, vgrad, mine, send = call(
+        functools.partial(value_kernel, count, shares),
+        (wide, shape((own, inner), bf16), narrow, narrow),
+        [VMEM] * (count + 1),
+        [pltpu.VMEM((rows, inner), bf16)],
+    )(probability, *all_projected)
+    received = rotated(send, "dp", 1)
+    result = call(
+        backward_kernel,
+        shape((frames, places, channels), bf16),
+        [VMEM] * 7 + [ANY] * 3,
+        [pltpu.VMEM((2, own, inner), bf16)] + held,
+    )(probability, queries, key_rows, values, joined, vgrad, upstream, *weights)
+    sent_grad = shifted(result, "pipe", -1)
+    value_part = call(
+        gradient_kernel, shape((inner // shares, channels), jnp.float32), [VMEM] * 4
+    )(flat, mine, other_flat, received)
+    return (sent_grad[None, None], value_part.T[None])
+
+
+def few_rows(mesh, acts, inner):
+    count, members = mesh.shape["frame"], mesh.shape["dp"]
+    rows = acts.shape[2] * acts.shape[3]
+    share = inner // (count * members)
+    return members == 2 and rows <= 128 and share <= 128 and HEADS % 2 == 0
+
+
 def solution(mesh):
-    return jax.shard_map(
-        body,
-        mesh=mesh,
-        in_specs=(
-            P("pipe", "dp", "frame", None, None),
-            P("pipe", "dp", "frame", None, None),
-            P("pipe", None, None),
-            P("pipe", None, None),
-            P("pipe", None, None),
-            P("pipe", None, None),
-        ),
-        out_specs=(P("pipe", "dp", "frame", None, None), P("pipe", None, ("frame", "dp"))),
-        check_vma=False,
-    )
+    specs = (P("pipe", "dp", "frame", None, None),) * 2 + (P("pipe", None, None),) * 4
+
+    def sharded(body):
+        return jax.shard_map(
+            body,
+            mesh=mesh,
+            in_specs=specs,
+            out_specs=(specs[0], P("pipe", None, ("frame", "dp"))),
+            check_vma=False,
+        )
+
+    def program(acts, cotangent, *weights):
+        if few_rows(mesh, acts, weights[0].shape[-1]):
+            return sharded(few_rows_body)(acts, cotangent, *weights)
+        return sharded(general_body)(acts, cotangent, *weights)
+
+    return program

time: 103 us -> 40.9 us (0.40)
  waiting for transfers between devices: 47.8 us -> 10.4 us
  between operations: 14.2 us -> 0.72 us
  matrix products: 9.96 us -> 0 us
  Pallas kernels: 0 us -> 8.8 us
  blocking collectives: 7.64 us -> 0 us
  other arithmetic: 2.47 us -> 0 us
    reduce_scatter x2 -> x0, waiting for transfers between devices: 39.4 us -> none  [the longest x1 39.4 us: body(): lax.psum_scatter(value_grad.astype(jnp.bfloat16), 'frame', scatter_dimens...]
    dot_general x12 -> x0, matrix products: 9.75 us -> none  [the longest x3 2.92 us: project_heads(): jnp.dot(inputs, weight, preferred_element_type=jnp.float32)]
    ppermute x0 -> x8, starting transfers between devices: none -> 9.06 us  [rotated(): lax.ppermute(shard, axis, [(i, (i + by) % count) for i in range(count)])]
    pallas_call x0 -> x6, Pallas kernels: none -> 8.8 us  [the longest x1 4.12 us: few_rows_body(): call(backward_kernel, shape((frames, places, channels), bf16), [VMEM] * 7...]
    all_to_all x2 -> x0, starting transfers between devices: 8.7 us -> none  [the longest x1 5.41 us: body(): lax.all_to_all(inputs, 'frame', split_axis=1, concat_axis=0, tiled=True)]
    all_to_all x1 -> x0, blocking collectives: 7.64 us -> none  [body(): lax.all_to_all(row_result, 'frame', split_axis=0, concat_axis=1, tiled=True)]
    ppermute x0 -> x8, waiting for transfers between devices: none -> 7.51 us  [rotated(): lax.ppermute(shard, axis, [(i, (i + by) % count) for i in range(count)])]
    all_to_all x2 -> x0, waiting for transfers between devices: 5.34 us -> none  [the longest x1 3.11 us: body(): lax.all_to_all(inputs, 'frame', split_axis=1, concat_axis=0, tiled=True)]
  transfers between devices with their start and end apart: 5 -> 9, of which waited for: 4 -> 3; matrix products, arithmetic and copies ran while one was open for 10% -> 0% of each run, Pallas kernels for 0% -> 19%
where the time goes in v1:
time: 40.9 us; the launch traced here: 40.3 us
  starting transfers between devices  13.3 us (33%)
  waiting for transfers between devices  10.4 us (25%)
  Pallas kernels  8.8 us (22%)
  local copies, waits for them, and re-layouts  7.05 us (17%)
  between operations  0.72 us (2%)
    ppermute x8, starting transfers between devices, rotated(): lax.ppermute(shard, axis, [(i, (i + by) % count) for i in range(count)])  9.06 us
    ppermute x8, waiting for transfers between devices, rotated(): lax.ppermute(shard, axis, [(i, (i + by) % count) for i in range(count)])  7.51 us
    unnamed x15, local copies, waits for them, and re-layouts  7.05 us
    ppermute x1, starting transfers between devices, shifted(): return lax.ppermute(shard, axis, pairs)  4.25 us
    pallas_call x1, Pallas kernels, few_rows_body(): call(backward_kernel, shape((frames, places, channels), bf16), [VMEM] * 7...  4.12 us
    ppermute x1, waiting for transfers between devices, shifted(): return lax.ppermute(shard, axis, pairs)  2.91 us
    pallas_call x1, Pallas kernels, few_rows_body(): call(functools.partial(forward_kernel, places), (wide, wide, wide, shape(...  2.6 us
    pallas_call x1, Pallas kernels, few_rows_body(): call(gradient_kernel, shape((inner // shares, channels), jnp.float32), [V...  1.13 us
  transfers between devices with their start and end apart: 9, of which 3 were waited for; matrix products, arithmetic and copies ran while one was open for 0% of the time, Pallas kernels for 19%

profile of v1, /device:TPU:1, one launch (start us, length us, event | category | flops | bytes accessed | tf_op | source)
XLA Modules:
  0.0 40.3 jit_solution(14183143823895329244)
XLA Ops:
  0.6 0.0 copy-start
  0.6 4.2 %collective-permute-start = (bf16[8,4,1280]{2,1,0:T(4,128)(2,1)}, bf16[8,4,1280]{2,1,0:T(4,128)(2,1)S(1)}, u32[]{:S(2)}, u32[]{:S(2)}) collective-permute-start(bf16[8,4,1280]{2,1,0:T(4,128)(2,1)} %bitcast.19), channel_id=1, source_target_pairs={{0,24},{8,0},{16,8},{24,16},{1,25},{9,1},{17,9},{25,17},{2,26},{10... | collective-permute-start | bytes 245768 | tf_op jit(solution)/shard_map/ppermute | solution.py:26
  4.8 0.0 collective-permute-start.1
  4.8 0.5 %collective-permute-start.2 = (bf16[8,4,1280]{2,1,0:T(4,128)(2,1)}, bf16[8,4,1280]{2,1,0:T(4,128)(2,1)S(1)}, u32[]{:S(2)}, u32[]{:S(2)}) collective-permute-start(bf16[8,4,1280]{2,1,0:T(4,128)(2,1)} %bitcast.21), channel_id=1, source_target_pairs={{0,8},{8,16},{16,24},{24,0},{1,9},{9,17},{17,25},{25,1},{2,10},{10... | collective-permute-start | bytes 245768 | tf_op jit(solution)/shard_map/ppermute | solution.py:26
  5.3 1.3 %collective-permute-done.refs_1_ = bf16[8,4,1280]{2,1,0:T(4,128)(2,1)S(1)} collective-permute-done((bf16[8,4,1280]{2,1,0:T(4,128)(2,1)}, bf16[8,4,1280]{2,1,0:T(4,128)(2,1)S(1)}, u32[]{:S(2)}, u32[]{:S(2)}) %collective-permute-start) | collective-permute-done | bytes 81952 | tf_op jit(solution)/shard_map/ppermute | solution.py:26
  6.6 6.2 %collective-permute-done.1.refs_2_ = bf16[8,4,1280]{2,1,0:T(4,128)(2,1)S(1)} collective-permute-done((bf16[8,4,1280]{2,1,0:T(4,128)(2,1)}, bf16[8,4,1280]{2,1,0:T(4,128)(2,1)S(1)}, u32[]{:S(2)}, u32[]{:S(2)}) %collective-permute-start.1) | collective-permute-done | bytes 81952 | tf_op jit(solution)/shard_map/ppermute | solution.py:26
  12.8 0.0 collective-permute-done.2.refs_3_
  12.8 0.9 %copy-done.6 = bf16[1,1,8,4,1280]{4,3,2,1,0:T(4,128)(2,1)S(1)} copy-done((bf16[1,1,8,4,1280]{4,3,2,1,0:T(4,128)(2,1)S(1)}, bf16[1,1,8,4,1280]{4,3,2,1,0:T(4,128)(2,1)}, u32[]{:S(2)}) %copy-start.6) | copy-done | bytes 81944
  13.7 0.1 shard_map.77.refs_0_.row_ref
  13.7 1.3 %collective-permute-start.7 = (bf16[128,1280]{1,0:T(8,128)(2,1)S(1)}, bf16[128,1280]{1,0:T(8,128)(2,1)S(1)}, u32[]{:S(2)}, u32[]{:S(2)}) collective-permute-start(bf16[128,1280]{1,0:T(8,128)(2,1)S(1)} %shard_map.77.refs_0_.row_ref), channel_id=1, source_target_pairs={{0,1},{1,0},{2,3},{3,2},{4,5},{5,4},{6,7},{7,6},{8,9},{9,8},{10,11... | collective-permute-start | bytes 983048 | tf_op jit(solution)/shard_map/ppermute | solution.py:26
  15.0 1.5 %copy-done.4 = bf16[1,1280,768]{2,1,0:T(8,128)(2,1)S(1)} copy-done((bf16[1,1280,768]{2,1,0:T(8,128)(2,1)S(1)}, bf16[1,1280,768]{2,1,0:T(8,128)(2,1)}, u32[]{:S(2)}) %copy-start.4) | copy-done | bytes 1966104
  16.6 0.9 %copy-done.5 = bf16[1,1,8,4,1280]{4,3,2,1,0:T(4,128)(2,1)S(1)} copy-done((bf16[1,1,8,4,1280]{4,3,2,1,0:T(4,128)(2,1)S(1)}, bf16[1,1,8,4,1280]{4,3,2,1,0:T(4,128)(2,1)}, u32[]{:S(2)}) %copy-start.5) | copy-done | bytes 81944
  17.5 0.4 %shard_map.79.refs_1_ = bf16[32,768]{1,0:T(8,128)(2,1)S(1)} custom-call(bf16[8,4,1280]{2,1,0:T(4,128)(2,1)S(1)} %bitcast.17, bf16[1280,768]{1,0:T(8,128)(2,1)S(1)} %bitcast.16), custom_call_target="tpu_custom_call" | custom-call | tf_op jit(solution)/shard_map/pallas_call | solution.py:273
  17.9 0.2 collective-permute-start.3
  18.1 1.3 %collective-permute-start.4 = (bf16[32,768]{1,0:T(8,128)(2,1)S(1)}, bf16[32,768]{1,0:T(8,128)(2,1)S(1)}, u32[]{:S(2)}, u32[]{:S(2)}) collective-permute-start(bf16[32,768]{1,0:T(8,128)(2,1)S(1)} %shard_map.79.refs_1_), channel_id=1, source_target_pairs={{0,16},{8,24},{16,0},{24,8},{1,17},{9,25},{17,1},{25,9},{2,18},{10... | collective-permute-start | bytes 147464 | tf_op jit(solution)/shard_map/ppermute | solution.py:26
  19.4 1.4 %collective-permute-start.5 = (bf16[32,768]{1,0:T(8,128)(2,1)S(1)}, bf16[32,768]{1,0:T(8,128)(2,1)S(1)}, u32[]{:S(2)}, u32[]{:S(2)}) collective-permute-start(bf16[32,768]{1,0:T(8,128)(2,1)S(1)} %shard_map.79.refs_1_), channel_id=1, source_target_pairs={{0,8},{8,16},{16,24},{24,0},{1,9},{9,17},{17,25},{25,1},{2,10},{10... | collective-permute-start | bytes 147464 | tf_op jit(solution)/shard_map/ppermute | solution.py:26
  20.7 0.0 copy-done
  20.7 1.5 %copy-done.1 = bf16[1,1280,768]{2,1,0:T(8,128)(2,1)S(1)} copy-done((bf16[1,1280,768]{2,1,0:T(8,128)(2,1)S(1)}, bf16[1,1280,768]{2,1,0:T(8,128)(2,1)}, u32[]{:S(2)}) %copy-start.1) | copy-done | bytes 1966104
  22.3 1.5 %copy-done.3 = bf16[1,1280,768]{2,1,0:T(8,128)(2,1)S(1)} copy-done((bf16[1,1280,768]{2,1,0:T(8,128)(2,1)S(1)}, bf16[1,1280,768]{2,1,0:T(8,128)(2,1)}, u32[]{:S(2)}) %copy-start.3) | copy-done | bytes 1966104
  23.8 2.6 %shard_map.78 = (bf16[128,768]{1,0:T(8,128)(2,1)S(1)}, bf16[128,768]{1,0:T(8,128)(2,1)S(1)}, bf16[128,768]{1,0:T(8,128)(2,1)S(1)}, f32[6,128,256]{2,1,0:T(8,128)S(1)}) custom-call(bf16[128,1280]{1,0:T(8,128)(2,1)S(1)} %shard_map.77.refs_0_.row_ref, bf16[1280,768]{1,0:T(8,128)(2,1)S(1)} %bitcast.10, bf16[1280,768]{1,0:T(8,128)(2,1)S(1)} %bitcast.12, ...), custom_call_target="tpu_custom_call" | custom-call | tf_op jit(solution)/shard_map/pallas_call | solution.py:278
  26.4 0.0 collective-permute-done.3.refs_2_
  26.5 0.0 collective-permute-done.4.refs_3_
  26.5 0.0 collective-permute-done.5.refs_4_
  26.5 0.5 %shard_map.80 = (bf16[128,768]{1,0:T(8,128)(2,1)S(1)}, bf16[32,768]{1,0:T(8,128)(2,1)S(1)}, bf16[128,128]{1,0:T(8,128)(2,1)S(1)}, bf16[128,128]{1,0:T(8,128)(2,1)S(1)}) custom-call(f32[6,128,256]{2,1,0:T(8,128)S(1)} %get-tuple-element.10.refs_0_, bf16[32,768]{1,0:T(8,128)(2,1)S(1)} %shard_map.79.refs_1_, bf16[32,768]{1,0:T(8,128)(2,1)S(1)} %collective-permute-done.3.refs_2_, ...), custom_call_target="tpu_custom_call" | custom-call | tf_op jit(solution)/shard_map/pallas_call | solution.py:285
  26.9 4.1 %shard_map.81 = bf16[8,4,1280]{2,1,0:T(4,128)(2,1)S(1)} custom-call(f32[6,128,256]{2,1,0:T(8,128)S(1)} %get-tuple-element.10.refs_0_, bf16[128,768]{1,0:T(8,128)(2,1)S(1)} %get-tuple-element.11.refs_1_, bf16[128,768]{1,0:T(8,128)(2,1)S(1)} %get-tuple-element.12.refs_2_, bf16[128,768]{1,0:T(8,128)(2,1)S(1)} %get-tuple-element.13.refs_3_, ...), custom_call_target="tpu_custom_call" | custom-call | tf_op jit(solution)/shard_map/pallas_call | solution.py:292
  31.1 4.2 %collective-permute-start.6 = (bf16[8,4,1280]{2,1,0:T(4,128)(2,1)S(1)}, bf16[8,4,1280]{2,1,0:T(4,128)(2,1)S(1)}, u32[]{:S(2)}, u32[]{:S(2)}) collective-permute-start(bf16[8,4,1280]{2,1,0:T(4,128)(2,1)S(1)} %shard_map.81), channel_id=1, source_target_pairs={{2,0},{4,2},{6,4},{3,1},{5,3},{7,5},{10,8},{12,10},{14,12},{11,9},... | collective-permute-start | bytes 245768 | tf_op jit(solution)/shard_map/ppermute | solution.py:21
  35.3 0.3 collective-permute-start.8
  35.6 2.9 %collective-permute-done.6 = bf16[8,4,1280]{2,1,0:T(4,128)(2,1)S(1)} collective-permute-done((bf16[8,4,1280]{2,1,0:T(4,128)(2,1)S(1)}, bf16[8,4,1280]{2,1,0:T(4,128)(2,1)S(1)}, u32[]{:S(2)}, u32[]{:S(2)}) %collective-permute-start.6) | collective-permute-done | bytes 81952 | tf_op jit(solution)/shard_map/ppermute | solution.py:21
  38.5 0.0 collective-permute-done.8.other_ref
  38.5 0.0 collective-permute-done.7.other_row_ref
  38.5 1.1 %shard_map.82 = f32[96,1280]{1,0:T(8,128)} custom-call(bf16[128,1280]{1,0:T(8,128)(2,1)S(1)} %shard_map.77.refs_0_.row_ref, bf16[128,128]{1,0:T(8,128)(2,1)S(1)} %get-tuple-element.16.mine_ref, bf16[128,1280]{1,0:T(8,128)(2,1)S(1)} %collective-permute-done.7.other_row_ref, bf16[128,128]{1,0:T(8,128)(2,1)S(1)} %collective-permute-done.8.other_ref), custom_call_target="tpu_custom_call" | custom-call | tf_op jit(solution)/shard_map/pallas_call | solution.py:299
  39.7 0.6 %copy.9 = bf16[1,1,8,4,1280]{4,3,2,1,0:T(4,128)(2,1)} copy(bf16[1,1,8,4,1280]{4,3,2,1,0:T(4,128)(2,1)S(1)} %bitcast.24) | data formatting | bytes 163840
  (7 shorter events, 0.0 us)
Async XLA Ops:
  0.6 20.1 %copy-start = (bf16[1,1280,768]{2,1,0:T(8,128)(2,1)S(1)}, bf16[1,1280,768]{2,1,0:T(8,128)(2,1)}, u32[]{:S(2)}) copy-start(bf16[1,1280,768]{2,1,0:T(8,128)(2,1)} %param.8) | copy-start | bytes 5898244
  0.6 6.0 %collective-permute-start = (bf16[8,4,1280]{2,1,0:T(4,128)(2,1)}, bf16[8,4,1280]{2,1,0:T(4,128)(2,1)S(1)}, u32[]{:S(2)}, u32[]{:S(2)}) collective-permute-start(bf16[8,4,1280]{2,1,0:T(4,128)(2,1)} %bitcast.19), channel_id=1, source_target_pairs={{0,24},{8,0},{16,8},{24,16},{1,25},{9,1},{17,9},{25,17},{2,26},{10... | collective-permute-start | bytes 245768 | tf_op jit(solution)/shard_map/ppermute | solution.py:26
  4.8 8.0 %collective-permute-start.1 = (bf16[8,4,1280]{2,1,0:T(4,128)(2,1)}, bf16[8,4,1280]{2,1,0:T(4,128)(2,1)S(1)}, u32[]{:S(2)}, u32[]{:S(2)}) collective-permute-start(bf16[8,4,1280]{2,1,0:T(4,128)(2,1)} %bitcast.20), channel_id=1, source_target_pairs={{0,16},{8,24},{16,0},{24,8},{1,17},{9,25},{17,1},{25,9},{2,18},{10... | collective-permute-start | bytes 245768 | tf_op jit(solution)/shard_map/ppermute | solution.py:26
  4.8 8.0 %collective-permute-start.2 = (bf16[8,4,1280]{2,1,0:T(4,128)(2,1)}, bf16[8,4,1280]{2,1,0:T(4,128)(2,1)S(1)}, u32[]{:S(2)}, u32[]{:S(2)}) collective-permute-start(bf16[8,4,1280]{2,1,0:T(4,128)(2,1)} %bitcast.21), channel_id=1, source_target_pairs={{0,8},{8,16},{16,24},{24,0},{1,9},{9,17},{17,25},{25,1},{2,10},{10... | collective-permute-start | bytes 245768 | tf_op jit(solution)/shard_map/ppermute | solution.py:26
  12.8 0.9 %copy-start.6 = (bf16[1,1,8,4,1280]{4,3,2,1,0:T(4,128)(2,1)S(1)}, bf16[1,1,8,4,1280]{4,3,2,1,0:T(4,128)(2,1)}, u32[]{:S(2)}) copy-start(bf16[1,1,8,4,1280]{4,3,2,1,0:T(4,128)(2,1)} %param.6) | copy-start | bytes 245764
  13.7 24.8 %collective-permute-start.7 = (bf16[128,1280]{1,0:T(8,128)(2,1)S(1)}, bf16[128,1280]{1,0:T(8,128)(2,1)S(1)}, u32[]{:S(2)}, u32[]{:S(2)}) collective-permute-start(bf16[128,1280]{1,0:T(8,128)(2,1)S(1)} %shard_map.77.refs_0_.row_ref), channel_id=1, source_target_pairs={{0,1},{1,0},{2,3},{3,2},{4,5},{5,4},{6,7},{7,6},{8,9},{9,8},{10,11... | collective-permute-start | bytes 983048 | tf_op jit(solution)/shard_map/ppermute | solution.py:26
  15.0 1.5 %copy-start.4 = (bf16[1,1280,768]{2,1,0:T(8,128)(2,1)S(1)}, bf16[1,1280,768]{2,1,0:T(8,128)(2,1)}, u32[]{:S(2)}) copy-start(bf16[1,1280,768]{2,1,0:T(8,128)(2,1)} %param.11) | copy-start | bytes 5898244
  16.6 0.9 %copy-start.5 = (bf16[1,1,8,4,1280]{4,3,2,1,0:T(4,128)(2,1)S(1)}, bf16[1,1,8,4,1280]{4,3,2,1,0:T(4,128)(2,1)}, u32[]{:S(2)}) copy-start(bf16[1,1,8,4,1280]{4,3,2,1,0:T(4,128)(2,1)} %param.7) | copy-start | bytes 245764
  17.9 8.5 %collective-permute-start.3 = (bf16[32,768]{1,0:T(8,128)(2,1)S(1)}, bf16[32,768]{1,0:T(8,128)(2,1)S(1)}, u32[]{:S(2)}, u32[]{:S(2)}) collective-permute-start(bf16[32,768]{1,0:T(8,128)(2,1)S(1)} %shard_map.79.refs_1_), channel_id=1, source_target_pairs={{0,24},{8,0},{16,8},{24,16},{1,25},{9,1},{17,9},{25,17},{2,26},{10... | collective-permute-start | bytes 147464 | tf_op jit(solution)/shard_map/ppermute | solution.py:26
  18.1 8.4 %collective-permute-start.4 = (bf16[32,768]{1,0:T(8,128)(2,1)S(1)}, bf16[32,768]{1,0:T(8,128)(2,1)S(1)}, u32[]{:S(2)}, u32[]{:S(2)}) collective-permute-start(bf16[32,768]{1,0:T(8,128)(2,1)S(1)} %shard_map.79.refs_1_), channel_id=1, source_target_pairs={{0,16},{8,24},{16,0},{24,8},{1,17},{9,25},{17,1},{25,9},{2,18},{10... | collective-permute-start | bytes 147464 | tf_op jit(solution)/shard_map/ppermute | solution.py:26
  19.4 7.1 %collective-permute-start.5 = (bf16[32,768]{1,0:T(8,128)(2,1)S(1)}, bf16[32,768]{1,0:T(8,128)(2,1)S(1)}, u32[]{:S(2)}, u32[]{:S(2)}) collective-permute-start(bf16[32,768]{1,0:T(8,128)(2,1)S(1)} %shard_map.79.refs_1_), channel_id=1, source_target_pairs={{0,8},{8,16},{16,24},{24,0},{1,9},{9,17},{17,25},{25,1},{2,10},{10... | collective-permute-start | bytes 147464 | tf_op jit(solution)/shard_map/ppermute | solution.py:26
  20.7 1.5 %copy-start.1 = (bf16[1,1280,768]{2,1,0:T(8,128)(2,1)S(1)}, bf16[1,1280,768]{2,1,0:T(8,128)(2,1)}, u32[]{:S(2)}) copy-start(bf16[1,1280,768]{2,1,0:T(8,128)(2,1)} %param.9) | copy-start | bytes 5898244
  22.3 1.5 %copy-start.3 = (bf16[1,1280,768]{2,1,0:T(8,128)(2,1)S(1)}, bf16[1,1280,768]{2,1,0:T(8,128)(2,1)}, u32[]{:S(2)}) copy-start(bf16[1,1280,768]{2,1,0:T(8,128)(2,1)} %param.10) | copy-start | bytes 5898244
  23.8 3.1 %copy-start.2 = (bf16[1,1280,768]{2,1,0:T(8,128)(2,1)S(1)}, bf16[1,1280,768]{2,1,0:T(8,128)(2,1)}, u32[]{:S(2)}) copy-start(bf16[1,1280,768]{2,1,0:T(8,128)(2,1)} %param.9) | copy-start | bytes 5898244
  31.1 7.5 %collective-permute-start.6 = (bf16[8,4,1280]{2,1,0:T(4,128)(2,1)S(1)}, bf16[8,4,1280]{2,1,0:T(4,128)(2,1)S(1)}, u32[]{:S(2)}, u32[]{:S(2)}) collective-permute-start(bf16[8,4,1280]{2,1,0:T(4,128)(2,1)S(1)} %shard_map.81), channel_id=1, source_target_pairs={{2,0},{4,2},{6,4},{3,1},{5,3},{7,5},{10,8},{12,10},{14,12},{11,9},... | collective-permute-start | bytes 245768 | tf_op jit(solution)/shard_map/ppermute | solution.py:21
  35.3 3.2 %collective-permute-start.8 = (bf16[128,128]{1,0:T(8,128)(2,1)S(1)}, bf16[128,128]{1,0:T(8,128)(2,1)S(1)}, u32[]{:S(2)}, u32[]{:S(2)}) collective-permute-start(bf16[128,128]{1,0:T(8,128)(2,1)S(1)} %get-tuple-element.17), channel_id=1, source_target_pairs={{0,1},{1,0},{2,3},{3,2},{4,5},{5,4},{6,7},{7,6},{8,9},{9,8},{10,11... | collective-permute-start | bytes 98312 | tf_op jit(solution)/shard_map/ppermute | solution.py:26

commit v2 on v1

--- a/solution.py
+++ b/solution.py
@@ -139,18 +139,22 @@
         out_ref[i * own : (i + 1) * own, :] = flat_rows(ref)
 
 
-def forward_kernel(places, *refs):
-    row_ref, *weight_refs = refs[:4]
-    q_ref, k_ref, v_ref, prob_ref, held, sems = refs[4:]
+def hold_kernel(*refs):
+    *weight_refs, held_ref, sems = refs
     copies = [
-        pltpu.make_async_copy(weight_refs[i], held.at[i], sems.at[i]) for i in range(3)
+        pltpu.make_async_copy(ref, held_ref.at[i], sems.at[i]) for i, ref in enumerate(weight_refs)
     ]
     for copy in copies:
         copy.start()
+    for copy in copies:
+        copy.wait()
+
+
+def forward_kernel(places, *refs):
+    row_ref, held_ref, q_ref, k_ref, v_ref, prob_ref = refs
     rows = row_ref[...]
     for i, out_ref in enumerate((q_ref, k_ref, v_ref)):
-        copies[i].wait()
-        out_ref[...] = dot_nn(rows, held[i]).astype(jnp.bfloat16)
+        out_ref[...] = dot_nn(rows, held_ref[i]).astype(jnp.bfloat16)
     count = rows.shape[0]
     row = lax.broadcasted_iota(jnp.int32, (count, 2 * count), 0)
     col = lax.broadcasted_iota(jnp.int32, (count, 2 * count), 1)
@@ -193,13 +197,8 @@
 
 
 def backward_kernel(*refs):
-    prob_ref, q_ref, k_ref, v_ref, proj_ref, vgrad_ref, upstream_ref, *weight_refs = refs[:10]
-    out_ref, grads, held, sems = refs[10:]
-    copies = [
-        pltpu.make_async_copy(weight_refs[i], held.at[i], sems.at[i]) for i in (2, 0, 1)
-    ]
-    for copy in copies:
-        copy.start()
+    prob_ref, q_ref, k_ref, v_ref, proj_ref, vgrad_ref, upstream_ref, held_ref = refs[:8]
+    out_ref, grads = refs[8:]
     count = proj_ref.shape[0]
     own = vgrad_ref.shape[0]
     width = 2 * HEAD_DIM
@@ -217,13 +216,10 @@
         second = dot_tn(score_grad[:, count : count + own], keys)
         query_grad = jnp.where(lane < HEAD_DIM, first, second) * score_scale
         grads[0, :, at] = query_grad.astype(jnp.bfloat16)
-    copies[0].wait()
-    branch = dot_nt(vgrad_ref[...], held[2])
-    copies[1].wait()
-    branch = branch + dot_nt(grads[0], held[0])
-    copies[2].wait()
-    branch = branch + dot_nt(grads[1], held[1])
-    branch = branch.astype(jnp.bfloat16).astype(jnp.float32)
+    branch = dot_nt(held_ref[2], vgrad_ref[...])
+    branch = branch + dot_nt(held_ref[0], grads[0])
+    branch = branch + dot_nt(held_ref[1], grads[1])
+    branch = branch.T.astype(jnp.bfloat16).astype(jnp.float32)
     result = flat_rows(upstream_ref).astype(jnp.float32) + branch
     out_ref[...] = result.reshape(out_ref.shape).astype(jnp.bfloat16)
 
@@ -234,7 +230,7 @@
 
 
 VMEM = pl.BlockSpec(memory_space=pltpu.VMEM)
-ANY = pl.BlockSpec(memory_space=pl.ANY)
+HBM = pl.BlockSpec(memory_space=pltpu.HBM)
 
 
 def call(kernel, out_shape, in_specs, scratch=(), grant=24):
@@ -261,7 +257,6 @@
     weights = (w_query[0], w_key[0], w_value[0])
     shape = jax.ShapeDtypeStruct
     turns = range(count - 1, 0, -1)
-    held = [pltpu.VMEM((3, channels, inner), bf16), pltpu.SemaphoreType.DMA((3,))]
 
     def gathered(block):
         received = [block]
@@ -272,15 +267,21 @@
     blocks = gathered(inputs)
     projected = call(project_kernel, shape((own, inner), bf16), [VMEM, VMEM])(upstream, w_out[0])
     all_projected = gathered(projected)
+    held = call(
+        hold_kernel,
+        shape((3, channels, inner), bf16),
+        [HBM] * 3,
+        [pltpu.SemaphoreType.DMA((3,))],
+        grant=54,
+    )(*weights)
     flat = call(flatten_kernel, shape((rows, channels), bf16), [VMEM] * count)(*blocks)
     other_flat = rotated(flat, "dp", 1)
     wide = shape((rows, inner), bf16)
     queries, key_rows, values, probability = call(
         functools.partial(forward_kernel, places),
         (wide, wide, wide, shape((HEADS // 2, rows, 2 * rows), jnp.float32)),
-        [VMEM] + [ANY] * 3,
-        held,
-    )(flat, *weights)
+        [VMEM] * 2,
+    )(flat, held)
     narrow = shape((rows, 128), bf16)
     joined, vgrad, mine, send = call(
         functools.partial(value_kernel, count, shares),
@@ -292,9 +293,9 @@
     result = call(
         backward_kernel,
         shape((frames, places, channels), bf16),
-        [VMEM] * 7 + [ANY] * 3,
-        [pltpu.VMEM((2, own, inner), bf16)] + held,
-    )(probability, queries, key_rows, values, joined, vgrad, upstream, *weights)
+        [VMEM] * 8,
+        [pltpu.VMEM((2, own, inner), bf16)],
+    )(probability, queries, key_rows, values, joined, vgrad, upstream, held)
     sent_grad = shifted(result, "pipe", -1)
     value_part = call(
         gradient_kernel, shape((inner // shares, channels), jnp.float32), [VMEM] * 4

time: 40.9 us -> 43.9 us (1.073)
  Pallas kernels: 8.8 us -> 11.2 us
  local copies, waits for them, and re-layouts: 7.05 us -> 7.64 us
    pallas_call x1 -> x2, Pallas kernels: 4.12 us -> 7.91 us  [the longest x1 5.28 us: few_rows_body(): call(hold_kernel, shape((3, channels, inner), bf16), [HBM] * 3, [pltpu.Se...]
    pallas_call x1, Pallas kernels: 2.6 us -> 1.15 us  [few_rows_body(): call(functools.partial(forward_kernel, places), (wide, wide, wide, shape(...]
    unnamed x15 -> x13, local copies, waits for them, and re-layouts: 7.05 us -> 7.64 us
  transfers between devices with their start and end apart: 9 -> 9, of which waited for: 3 -> 3; matrix products, arithmetic and copies ran while one was open for 0% -> 0% of each run, Pallas kernels for 19% -> 23%
where the time goes in v2:
time: 43.9 us; the launch traced here: 43.2 us
  starting transfers between devices  13.3 us (30%)
  Pallas kernels  11.2 us (26%)
  waiting for transfers between devices  10.4 us (24%)
  local copies, waits for them, and re-layouts  7.64 us (17%)
  between operations  0.71 us (2%)
    ppermute x8, starting transfers between devices, rotated(): lax.ppermute(shard, axis, [(i, (i + by) % count) for i in range(count)])  9.06 us
    unnamed x13, local copies, waits for them, and re-layouts  7.64 us
    ppermute x8, waiting for transfers between devices, rotated(): lax.ppermute(shard, axis, [(i, (i + by) % count) for i in range(count)])  7.51 us
    pallas_call x1, Pallas kernels, few_rows_body(): call(hold_kernel, shape((3, channels, inner), bf16), [HBM] * 3, [pltpu.Se...  5.28 us
    ppermute x1, starting transfers between devices, shifted(): return lax.ppermute(shard, axis, pairs)  4.25 us
    ppermute x1, waiting for transfers between devices, shifted(): return lax.ppermute(shard, axis, pairs)  2.91 us
    pallas_call x1, Pallas kernels, few_rows_body(): call(backward_kernel, shape((frames, places, channels), bf16), [VMEM] * 8...  2.63 us
    pallas_call x1, Pallas kernels, few_rows_body(): call(functools.partial(forward_kernel, places), (wide, wide, wide, shape(...  1.15 us
  transfers between devices with their start and end apart: 9, of which 3 were waited for; matrix products, arithmetic and copies ran while one was open for 0% of the time, Pallas kernels for 23%

profile of v2, /device:TPU:1, one launch (start us, length us, event | category | flops | bytes accessed | tf_op | source)
XLA Modules:
  0.0 43.2 jit_solution(12148434944948509063)
XLA Ops:
  0.6 4.2 %collective-permute-start = (bf16[8,4,1280]{2,1,0:T(4,128)(2,1)}, bf16[8,4,1280]{2,1,0:T(4,128)(2,1)S(1)}, u32[]{:S(2)}, u32[]{:S(2)}) collective-permute-start(bf16[8,4,1280]{2,1,0:T(4,128)(2,1)} %bitcast.13), channel_id=1, source_target_pairs={{0,24},{8,0},{16,8},{24,16},{1,25},{9,1},{17,9},{25,17},{2,26},{10... | collective-permute-start | bytes 245768 | tf_op jit(solution)/shard_map/ppermute | solution.py:26
  4.8 0.0 collective-permute-start.1
  4.8 0.5 %collective-permute-start.2 = (bf16[8,4,1280]{2,1,0:T(4,128)(2,1)}, bf16[8,4,1280]{2,1,0:T(4,128)(2,1)S(1)}, u32[]{:S(2)}, u32[]{:S(2)}) collective-permute-start(bf16[8,4,1280]{2,1,0:T(4,128)(2,1)} %bitcast.15), channel_id=1, source_target_pairs={{0,8},{8,16},{16,24},{24,0},{1,9},{9,17},{17,25},{25,1},{2,10},{10... | collective-permute-start | bytes 245768 | tf_op jit(solution)/shard_map/ppermute | solution.py:26
  5.3 1.3 %collective-permute-done.refs_1_ = bf16[8,4,1280]{2,1,0:T(4,128)(2,1)S(1)} collective-permute-done((bf16[8,4,1280]{2,1,0:T(4,128)(2,1)}, bf16[8,4,1280]{2,1,0:T(4,128)(2,1)S(1)}, u32[]{:S(2)}, u32[]{:S(2)}) %collective-permute-start) | collective-permute-done | bytes 81952 | tf_op jit(solution)/shard_map/ppermute | solution.py:26
  6.6 6.2 %collective-permute-done.1.refs_2_ = bf16[8,4,1280]{2,1,0:T(4,128)(2,1)S(1)} collective-permute-done((bf16[8,4,1280]{2,1,0:T(4,128)(2,1)}, bf16[8,4,1280]{2,1,0:T(4,128)(2,1)S(1)}, u32[]{:S(2)}, u32[]{:S(2)}) %collective-permute-start.1) | collective-permute-done | bytes 81952 | tf_op jit(solution)/shard_map/ppermute | solution.py:26
  12.8 0.0 collective-permute-done.2.refs_3_
  12.8 0.9 %copy-done.5 = bf16[1,1,8,4,1280]{4,3,2,1,0:T(4,128)(2,1)S(1)} copy-done((bf16[1,1,8,4,1280]{4,3,2,1,0:T(4,128)(2,1)S(1)}, bf16[1,1,8,4,1280]{4,3,2,1,0:T(4,128)(2,1)}, u32[]{:S(2)}) %copy-start.5) | copy-done | bytes 81944
  13.7 0.1 shard_map.77.refs_0_.row_ref
  13.7 1.3 %collective-permute-start.7 = (bf16[128,1280]{1,0:T(8,128)(2,1)S(1)}, bf16[128,1280]{1,0:T(8,128)(2,1)S(1)}, u32[]{:S(2)}, u32[]{:S(2)}) collective-permute-start(bf16[128,1280]{1,0:T(8,128)(2,1)S(1)} %shard_map.77.refs_0_.row_ref), channel_id=1, source_target_pairs={{0,1},{1,0},{2,3},{3,2},{4,5},{5,4},{6,7},{7,6},{8,9},{9,8},{10,11... | collective-permute-start | bytes 983048 | tf_op jit(solution)/shard_map/ppermute | solution.py:26
  15.0 1.5 %copy-done.2 = bf16[1,1280,768]{2,1,0:T(8,128)(2,1)S(1)} copy-done((bf16[1,1280,768]{2,1,0:T(8,128)(2,1)S(1)}, bf16[1,1280,768]{2,1,0:T(8,128)(2,1)}, u32[]{:S(2)}) %copy-start.2) | copy-done | bytes 1966104
  16.6 0.9 %copy-done.3 = bf16[1,1,8,4,1280]{4,3,2,1,0:T(4,128)(2,1)S(1)} copy-done((bf16[1,1,8,4,1280]{4,3,2,1,0:T(4,128)(2,1)S(1)}, bf16[1,1,8,4,1280]{4,3,2,1,0:T(4,128)(2,1)}, u32[]{:S(2)}) %copy-start.3) | copy-done | bytes 81944
  17.5 0.4 %shard_map.80.refs_1_ = bf16[32,768]{1,0:T(8,128)(2,1)S(1)} custom-call(bf16[8,4,1280]{2,1,0:T(4,128)(2,1)S(1)} %bitcast.11, bf16[1280,768]{1,0:T(8,128)(2,1)S(1)} %bitcast.10), custom_call_target="tpu_custom_call" | custom-call | tf_op jit(solution)/shard_map/pallas_call | solution.py:268
  17.9 0.2 collective-permute-start.3
  18.1 1.3 %collective-permute-start.4 = (bf16[32,768]{1,0:T(8,128)(2,1)S(1)}, bf16[32,768]{1,0:T(8,128)(2,1)S(1)}, u32[]{:S(2)}, u32[]{:S(2)}) collective-permute-start(bf16[32,768]{1,0:T(8,128)(2,1)S(1)} %shard_map.80.refs_1_), channel_id=1, source_target_pairs={{0,16},{8,24},{16,0},{24,8},{1,17},{9,25},{17,1},{25,9},{2,18},{10... | collective-permute-start | bytes 147464 | tf_op jit(solution)/shard_map/ppermute | solution.py:26
  19.3 1.4 %collective-permute-start.5 = (bf16[32,768]{1,0:T(8,128)(2,1)S(1)}, bf16[32,768]{1,0:T(8,128)(2,1)S(1)}, u32[]{:S(2)}, u32[]{:S(2)}) collective-permute-start(bf16[32,768]{1,0:T(8,128)(2,1)S(1)} %shard_map.80.refs_1_), channel_id=1, source_target_pairs={{0,8},{8,16},{16,24},{24,0},{1,9},{9,17},{17,25},{25,1},{2,10},{10... | collective-permute-start | bytes 147464 | tf_op jit(solution)/shard_map/ppermute | solution.py:26
  20.7 5.3 %shard_map.78.refs_1_.refs_7_ = bf16[3,1280,768]{2,1,0:T(8,128)(2,1)} custom-call(bf16[1280,768]{1,0:T(8,128)(2,1)} %bitcast.17, bf16[1280,768]{1,0:T(8,128)(2,1)} %bitcast.18, bf16[1280,768]{1,0:T(8,128)(2,1)} %bitcast.19), custom_call_target="tpu_custom_call" | custom-call | tf_op jit(solution)/shard_map/pallas_call | solution.py:270
  26.0 0.0 copy-start
  26.0 2.7 %copy-done = bf16[3,1280,768]{2,1,0:T(8,128)(2,1)S(1)} copy-done((bf16[3,1280,768]{2,1,0:T(8,128)(2,1)S(1)}, bf16[3,1280,768]{2,1,0:T(8,128)(2,1)}, u32[]{:S(2)}) %copy-start) | copy-done | bytes 5898264
  28.7 1.2 %shard_map.79 = (bf16[128,768]{1,0:T(8,128)(2,1)S(1)}, bf16[128,768]{1,0:T(8,128)(2,1)S(1)}, bf16[128,768]{1,0:T(8,128)(2,1)S(1)}, f32[6,128,256]{2,1,0:T(8,128)S(1)}) custom-call(bf16[128,1280]{1,0:T(8,128)(2,1)S(1)} %shard_map.77.refs_0_.row_ref, bf16[3,1280,768]{2,1,0:T(8,128)(2,1)S(1)} %copy-done), custom_call_target="tpu_custom_call" | custom-call | tf_op jit(solution)/shard_map/pallas_call | solution.py:280
  29.9 0.0 collective-permute-done.3.refs_2_
  29.9 0.0 collective-permute-done.4.refs_3_
  29.9 0.0 collective-permute-done.5.refs_4_
  29.9 0.5 %shard_map.81 = (bf16[128,768]{1,0:T(8,128)(2,1)S(1)}, bf16[32,768]{1,0:T(8,128)(2,1)S(1)}, bf16[128,128]{1,0:T(8,128)(2,1)S(1)}, bf16[128,128]{1,0:T(8,128)(2,1)S(1)}) custom-call(f32[6,128,256]{2,1,0:T(8,128)S(1)} %get-tuple-element.10.refs_0_, bf16[32,768]{1,0:T(8,128)(2,1)S(1)} %shard_map.80.refs_1_, bf16[32,768]{1,0:T(8,128)(2,1)S(1)} %collective-permute-done.3.refs_2_, ...), custom_call_target="tpu_custom_call" | custom-call | tf_op jit(solution)/shard_map/pallas_call | solution.py:286
  30.4 1.0 %copy-done.1 = bf16[3,1280,768]{2,1,0:T(8,128)(2,1)S(1)} copy-done((bf16[3,1280,768]{2,1,0:T(8,128)(2,1)S(1)}, bf16[3,1280,768]{2,1,0:T(8,128)(2,1)}, u32[]{:S(2)}) %copy-start.1) | copy-done | bytes 5898264
  31.4 2.6 %shard_map.82 = bf16[8,4,1280]{2,1,0:T(4,128)(2,1)S(1)} custom-call(f32[6,128,256]{2,1,0:T(8,128)S(1)} %get-tuple-element.10.refs_0_, bf16[128,768]{1,0:T(8,128)(2,1)S(1)} %get-tuple-element.11.refs_1_, bf16[128,768]{1,0:T(8,128)(2,1)S(1)} %get-tuple-element.12.refs_2_, bf16[128,768]{1,0:T(8,128)(2,1)S(1)} %get-tuple-element.13.refs_3_, ...), custom_call_target="tpu_custom_call" | custom-call | tf_op jit(solution)/shard_map/pallas_call | solution.py:293
  34.0 4.3 %collective-permute-start.6 = (bf16[8,4,1280]{2,1,0:T(4,128)(2,1)S(1)}, bf16[8,4,1280]{2,1,0:T(4,128)(2,1)S(1)}, u32[]{:S(2)}, u32[]{:S(2)}) collective-permute-start(bf16[8,4,1280]{2,1,0:T(4,128)(2,1)S(1)} %shard_map.82), channel_id=1, source_target_pairs={{2,0},{4,2},{6,4},{3,1},{5,3},{7,5},{10,8},{12,10},{14,12},{11,9},... | collective-permute-start | bytes 245768 | tf_op jit(solution)/shard_map/ppermute | solution.py:21
  38.3 0.3 collective-permute-start.8
  38.6 2.9 %collective-permute-done.6 = bf16[8,4,1280]{2,1,0:T(4,128)(2,1)S(1)} collective-permute-done((bf16[8,4,1280]{2,1,0:T(4,128)(2,1)S(1)}, bf16[8,4,1280]{2,1,0:T(4,128)(2,1)S(1)}, u32[]{:S(2)}, u32[]{:S(2)}) %collective-permute-start.6) | collective-permute-done | bytes 81952 | tf_op jit(solution)/shard_map/ppermute | solution.py:21
  41.5 0.0 collective-permute-done.8.other_ref
  41.5 0.0 collective-permute-done.7.other_row_ref
  41.5 1.1 %shard_map.83 = f32[96,1280]{1,0:T(8,128)} custom-call(bf16[128,1280]{1,0:T(8,128)(2,1)S(1)} %shard_map.77.refs_0_.row_ref, bf16[128,128]{1,0:T(8,128)(2,1)S(1)} %get-tuple-element.16.mine_ref, bf16[128,1280]{1,0:T(8,128)(2,1)S(1)} %collective-permute-done.7.other_row_ref, bf16[128,128]{1,0:T(8,128)(2,1)S(1)} %collective-permute-done.8.other_ref), custom_call_target="tpu_custom_call" | custom-call | tf_op jit(solution)/shard_map/pallas_call | solution.py:300
  42.6 0.6 %copy.9 = bf16[1,1,8,4,1280]{4,3,2,1,0:T(4,128)(2,1)} copy(bf16[1,1,8,4,1280]{4,3,2,1,0:T(4,128)(2,1)S(1)} %bitcast.21) | data formatting | bytes 163840
  (6 shorter events, 0.0 us)
Async XLA Ops:
  0.6 6.0 %collective-permute-start = (bf16[8,4,1280]{2,1,0:T(4,128)(2,1)}, bf16[8,4,1280]{2,1,0:T(4,128)(2,1)S(1)}, u32[]{:S(2)}, u32[]{:S(2)}) collective-permute-start(bf16[8,4,1280]{2,1,0:T(4,128)(2,1)} %bitcast.13), channel_id=1, source_target_pairs={{0,24},{8,0},{16,8},{24,16},{1,25},{9,1},{17,9},{25,17},{2,26},{10... | collective-permute-start | bytes 245768 | tf_op jit(solution)/shard_map/ppermute | solution.py:26
  4.8 8.0 %collective-permute-start.1 = (bf16[8,4,1280]{2,1,0:T(4,128)(2,1)}, bf16[8,4,1280]{2,1,0:T(4,128)(2,1)S(1)}, u32[]{:S(2)}, u32[]{:S(2)}) collective-permute-start(bf16[8,4,1280]{2,1,0:T(4,128)(2,1)} %bitcast.14), channel_id=1, source_target_pairs={{0,16},{8,24},{16,0},{24,8},{1,17},{9,25},{17,1},{25,9},{2,18},{10... | collective-permute-start | bytes 245768 | tf_op jit(solution)/shard_map/ppermute | solution.py:26
  4.8 8.0 %collective-permute-start.2 = (bf16[8,4,1280]{2,1,0:T(4,128)(2,1)}, bf16[8,4,1280]{2,1,0:T(4,128)(2,1)S(1)}, u32[]{:S(2)}, u32[]{:S(2)}) collective-permute-start(bf16[8,4,1280]{2,1,0:T(4,128)(2,1)} %bitcast.15), channel_id=1, source_target_pairs={{0,8},{8,16},{16,24},{24,0},{1,9},{9,17},{17,25},{25,1},{2,10},{10... | collective-permute-start | bytes 245768 | tf_op jit(solution)/shard_map/ppermute | solution.py:26
  12.8 0.9 %copy-start.5 = (bf16[1,1,8,4,1280]{4,3,2,1,0:T(4,128)(2,1)S(1)}, bf16[1,1,8,4,1280]{4,3,2,1,0:T(4,128)(2,1)}, u32[]{:S(2)}) copy-start(bf16[1,1,8,4,1280]{4,3,2,1,0:T(4,128)(2,1)} %param.6) | copy-start | bytes 245764
  13.7 27.8 %collective-permute-start.7 = (bf16[128,1280]{1,0:T(8,128)(2,1)S(1)}, bf16[128,1280]{1,0:T(8,128)(2,1)S(1)}, u32[]{:S(2)}, u32[]{:S(2)}) collective-permute-start(bf16[128,1280]{1,0:T(8,128)(2,1)S(1)} %shard_map.77.refs_0_.row_ref), channel_id=1, source_target_pairs={{0,1},{1,0},{2,3},{3,2},{4,5},{5,4},{6,7},{7,6},{8,9},{9,8},{10,11... | collective-permute-start | bytes 983048 | tf_op jit(solution)/shard_map/ppermute | solution.py:26
  15.0 1.5 %copy-start.2 = (bf16[1,1280,768]{2,1,0:T(8,128)(2,1)S(1)}, bf16[1,1280,768]{2,1,0:T(8,128)(2,1)}, u32[]{:S(2)}) copy-start(bf16[1,1280,768]{2,1,0:T(8,128)(2,1)} %param.11) | copy-start | bytes 5898244
  16.6 0.9 %copy-start.3 = (bf16[1,1,8,4,1280]{4,3,2,1,0:T(4,128)(2,1)S(1)}, bf16[1,1,8,4,1280]{4,3,2,1,0:T(4,128)(2,1)}, u32[]{:S(2)}) copy-start(bf16[1,1,8,4,1280]{4,3,2,1,0:T(4,128)(2,1)} %param.7) | copy-start | bytes 245764
  17.9 11.9 %collective-permute-start.3 = (bf16[32,768]{1,0:T(8,128)(2,1)S(1)}, bf16[32,768]{1,0:T(8,128)(2,1)S(1)}, u32[]{:S(2)}, u32[]{:S(2)}) collective-permute-start(bf16[32,768]{1,0:T(8,128)(2,1)S(1)} %shard_map.80.refs_1_), channel_id=1, source_target_pairs={{0,24},{8,0},{16,8},{24,16},{1,25},{9,1},{17,9},{25,17},{2,26},{10... | collective-permute-start | bytes 147464 | tf_op jit(solution)/shard_map/ppermute | solution.py:26
  18.1 11.8 %collective-permute-start.4 = (bf16[32,768]{1,0:T(8,128)(2,1)S(1)}, bf16[32,768]{1,0:T(8,128)(2,1)S(1)}, u32[]{:S(2)}, u32[]{:S(2)}) collective-permute-start(bf16[32,768]{1,0:T(8,128)(2,1)S(1)} %shard_map.80.refs_1_), channel_id=1, source_target_pairs={{0,16},{8,24},{16,0},{24,8},{1,17},{9,25},{17,1},{25,9},{2,18},{10... | collective-permute-start | bytes 147464 | tf_op jit(solution)/shard_map/ppermute | solution.py:26
  19.3 10.5 %collective-permute-start.5 = (bf16[32,768]{1,0:T(8,128)(2,1)S(1)}, bf16[32,768]{1,0:T(8,128)(2,1)S(1)}, u32[]{:S(2)}, u32[]{:S(2)}) collective-permute-start(bf16[32,768]{1,0:T(8,128)(2,1)S(1)} %shard_map.80.refs_1_), channel_id=1, source_target_pairs={{0,8},{8,16},{16,24},{24,0},{1,9},{9,17},{17,25},{25,1},{2,10},{10... | collective-permute-start | bytes 147464 | tf_op jit(solution)/shard_map/ppermute | solution.py:26
  26.0 2.7 %copy-start = (bf16[3,1280,768]{2,1,0:T(8,128)(2,1)S(1)}, bf16[3,1280,768]{2,1,0:T(8,128)(2,1)}, u32[]{:S(2)}) copy-start(bf16[3,1280,768]{2,1,0:T(8,128)(2,1)} %shard_map.78.refs_1_.refs_7_) | copy-start | bytes 17694724
  28.7 2.7 %copy-start.1 = (bf16[3,1280,768]{2,1,0:T(8,128)(2,1)S(1)}, bf16[3,1280,768]{2,1,0:T(8,128)(2,1)}, u32[]{:S(2)}) copy-start(bf16[3,1280,768]{2,1,0:T(8,128)(2,1)} %shard_map.78.refs_1_.refs_7_) | copy-start | bytes 17694724
  28.7 2.7 %copy-start.4 = (bf16[1,1,8,4,1280]{4,3,2,1,0:T(4,128)(2,1)S(1)}, bf16[1,1,8,4,1280]{4,3,2,1,0:T(4,128)(2,1)}, u32[]{:S(2)}) copy-start(bf16[1,1,8,4,1280]{4,3,2,1,0:T(4,128)(2,1)} %param.7) | copy-start | bytes 245764
  34.0 7.5 %collective-permute-start.6 = (bf16[8,4,1280]{2,1,0:T(4,128)(2,1)S(1)}, bf16[8,4,1280]{2,1,0:T(4,128)(2,1)S(1)}, u32[]{:S(2)}, u32[]{:S(2)}) collective-permute-start(bf16[8,4,1280]{2,1,0:T(4,128)(2,1)S(1)} %shard_map.82), channel_id=1, source_target_pairs={{2,0},{4,2},{6,4},{3,1},{5,3},{7,5},{10,8},{12,10},{14,12},{11,9},... | collective-permute-start | bytes 245768 | tf_op jit(solution)/shard_map/ppermute | solution.py:21
  38.3 3.2 %collective-permute-start.8 = (bf16[128,128]{1,0:T(8,128)(2,1)S(1)}, bf16[128,128]{1,0:T(8,128)(2,1)S(1)}, u32[]{:S(2)}, u32[]{:S(2)}) collective-permute-start(bf16[128,128]{1,0:T(8,128)(2,1)S(1)} %get-tuple-element.17), channel_id=1, source_target_pairs={{0,1},{1,0},{2,3},{3,2},{4,5},{5,4},{6,7},{7,6},{8,9},{9,8},{10,11... | collective-permute-start | bytes 98312 | tf_op jit(solution)/shard_map/ppermute | solution.py:26

commit v3 on v2

--- a/solution.py
+++ b/solution.py
@@ -120,8 +120,22 @@
     return lax.dot_general(a, b, (((0,), (0,)), ((), ())), preferred_element_type=jnp.float32)
 
 
-def project_kernel(upstream_ref, weight_ref, out_ref):
-    out_ref[...] = dot_nn(flat_rows(upstream_ref), weight_ref[...]).astype(jnp.bfloat16)
+def project_kernel(upstream_ref, *refs):
+    *weight_refs, out_ref, row_ref, held_ref, first, upstream, sems = refs
+    sources = [upstream_ref, *weight_refs]
+    targets = [upstream, first] + [held_ref.at[i] for i in range(3)]
+    copies = [
+        pltpu.make_async_copy(source, target, sems.at[i])
+        for i, (source, target) in enumerate(zip(sources, targets))
+    ]
+    for copy in copies:
+        copy.start()
+    copies[0].wait()
+    row_ref[...] = flat_rows(upstream)
+    copies[1].wait()
+    out_ref[...] = dot_nn(row_ref[...], first[...]).astype(jnp.bfloat16)
+    for copy in copies[2:]:
+        copy.wait()
 
 
 def pair_rows(pair):
@@ -137,17 +151,6 @@
     own = out_ref.shape[0] // len(act_refs)
     for i, ref in enumerate(act_refs):
         out_ref[i * own : (i + 1) * own, :] = flat_rows(ref)
-
-
-def hold_kernel(*refs):
-    *weight_refs, held_ref, sems = refs
-    copies = [
-        pltpu.make_async_copy(ref, held_ref.at[i], sems.at[i]) for i, ref in enumerate(weight_refs)
-    ]
-    for copy in copies:
-        copy.start()
-    for copy in copies:
-        copy.wait()
 
 
 def forward_kernel(places, *refs):
@@ -220,7 +223,7 @@
     branch = branch + dot_nt(held_ref[0], grads[0])
     branch = branch + dot_nt(held_ref[1], grads[1])
     branch = branch.T.astype(jnp.bfloat16).astype(jnp.float32)
-    result = flat_rows(upstream_ref).astype(jnp.float32) + branch
+    result = upstream_ref[...].astype(jnp.float32) + branch
     out_ref[...] = result.reshape(out_ref.shape).astype(jnp.bfloat16)
 
 
@@ -254,7 +257,7 @@
     own = frames * places
     rows = count * own
     bf16 = jnp.bfloat16
-    weights = (w_query[0], w_key[0], w_value[0])
+    weights = (w_out[0], w_query[0], w_key[0], w_value[0])
     shape = jax.ShapeDtypeStruct
     turns = range(count - 1, 0, -1)
 
@@ -265,15 +268,22 @@
         return received
 
     blocks = gathered(inputs)
-    projected = call(project_kernel, shape((own, inner), bf16), [VMEM, VMEM])(upstream, w_out[0])
+    hbm_args = [pltpu.with_memory_space_constraint(x, pltpu.HBM) for x in (upstream, *weights)]
+    projected, upstream_rows, held = call(
+        project_kernel,
+        (
+            shape((own, inner), bf16),
+            shape((own, channels), bf16),
+            pltpu.VMEM((3, channels, inner), bf16),
+        ),
+        [HBM] * 5,
+        [
+            pltpu.VMEM((channels, inner), bf16),
+            pltpu.VMEM(upstream.shape, bf16),
+            pltpu.SemaphoreType.DMA((5,)),
+        ],
+    )(*hbm_args)
     all_projected = gathered(projected)
-    held = call(
-        hold_kernel,
-        shape((3, channels, inner), bf16),
-        [HBM] * 3,
-        [pltpu.SemaphoreType.DMA((3,))],
-        grant=54,
-    )(*weights)
     flat = call(flatten_kernel, shape((rows, channels), bf16), [VMEM] * count)(*blocks)
     other_flat = rotated(flat, "dp", 1)
     wide = shape((rows, inner), bf16)
@@ -295,7 +305,7 @@
         shape((frames, places, channels), bf16),
         [VMEM] * 8,
         [pltpu.VMEM((2, own, inner), bf16)],
-    )(probability, queries, key_rows, values, joined, vgrad, upstream, held)
+    )(probability, queries, key_rows, values, joined, vgrad, upstream_rows, held)
     sent_grad = shifted(result, "pipe", -1)
     value_part = call(
         gradient_kernel, shape((inner // shares, channels), jnp.float32), [VMEM] * 4

time: 43.9 us -> 38 us (0.87)
  local copies, waits for them, and re-layouts: 7.64 us -> 1.52 us
  waiting for transfers between devices: 10.4 us -> 13.1 us
  Pallas kernels: 11.2 us -> 8.81 us
    unnamed x13 -> x3, local copies, waits for them, and re-layouts: 7.64 us -> 1.52 us
    ppermute x8, waiting for transfers between devices: 7.51 us -> 10.2 us  [rotated(): lax.ppermute(shard, axis, [(i, (i + by) % count) for i in range(count)])]
    pallas_call x2 -> x1, Pallas kernels: 5.73 us -> 3.39 us  [few_rows_body(): call(project_kernel, (shape((own, inner), bf16), shape((own, channels), b...]
  transfers between devices with their start and end apart: 9 -> 9, of which waited for: 3 -> 4; matrix products, arithmetic and copies ran while one was open for 0% -> 0% of each run, Pallas kernels for 23% -> 20%
where the time goes in v3:
time: 38 us; the launch traced here: 37.6 us
  starting transfers between devices  13.4 us (35%)
  waiting for transfers between devices  13.1 us (34%)
  Pallas kernels  8.81 us (23%)
  local copies, waits for them, and re-layouts  1.52 us (4%)
  between operations  0.69 us (2%)
    ppermute x8, waiting for transfers between devices, rotated(): lax.ppermute(shard, axis, [(i, (i + by) % count) for i in range(count)])  10.2 us
    ppermute x8, starting transfers between devices, rotated(): lax.ppermute(shard, axis, [(i, (i + by) % count) for i in range(count)])  9.09 us
    ppermute x1, starting transfers between devices, shifted(): return lax.ppermute(shard, axis, pairs)  4.31 us
    pallas_call x1, Pallas kernels, few_rows_body(): call(project_kernel, (shape((own, inner), bf16), shape((own, channels), b...  3.39 us
    ppermute x1, waiting for transfers between devices, shifted(): return lax.ppermute(shard, axis, pairs)  2.92 us
    pallas_call x1, Pallas kernels, few_rows_body(): call(backward_kernel, shape((frames, places, channels), bf16), [VMEM] * 8...  2.64 us
    unnamed x3, local copies, waits for them, and re-layouts  1.52 us
    pallas_call x1, Pallas kernels, few_rows_body(): call(functools.partial(forward_kernel, places), (wide, wide, wide, shape(...  1.15 us
  transfers between devices with their start and end apart: 9, of which 4 were waited for; matrix products, arithmetic and copies ran while one was open for 0% of the time, Pallas kernels for 20%

profile of v3, /device:TPU:1, one launch (start us, length us, event | category | flops | bytes accessed | tf_op | source)
XLA Modules:
  0.0 37.6 jit_solution(55543258190160839)
XLA Ops:
  0.6 4.2 %collective-permute-start = (bf16[8,4,1280]{2,1,0:T(4,128)(2,1)}, bf16[8,4,1280]{2,1,0:T(4,128)(2,1)S(1)}, u32[]{:S(2)}, u32[]{:S(2)}) collective-permute-start(bf16[8,4,1280]{2,1,0:T(4,128)(2,1)} %bitcast.10), channel_id=1, source_target_pairs={{0,24},{8,0},{16,8},{24,16},{1,25},{9,1},{17,9},{25,17},{2,26},{10... | collective-permute-start | bytes 245768 | tf_op jit(solution)/shard_map/ppermute | solution.py:26
  4.8 0.0 collective-permute-start.1
  4.8 0.5 %collective-permute-start.2 = (bf16[8,4,1280]{2,1,0:T(4,128)(2,1)}, bf16[8,4,1280]{2,1,0:T(4,128)(2,1)S(1)}, u32[]{:S(2)}, u32[]{:S(2)}) collective-permute-start(bf16[8,4,1280]{2,1,0:T(4,128)(2,1)} %bitcast.12), channel_id=1, source_target_pairs={{0,8},{8,16},{16,24},{24,0},{1,9},{9,17},{17,25},{25,1},{2,10},{10... | collective-permute-start | bytes 245768 | tf_op jit(solution)/shard_map/ppermute | solution.py:26
  5.3 1.3 %collective-permute-done.refs_1_ = bf16[8,4,1280]{2,1,0:T(4,128)(2,1)S(1)} collective-permute-done((bf16[8,4,1280]{2,1,0:T(4,128)(2,1)}, bf16[8,4,1280]{2,1,0:T(4,128)(2,1)S(1)}, u32[]{:S(2)}, u32[]{:S(2)}) %collective-permute-start) | collective-permute-done | bytes 81952 | tf_op jit(solution)/shard_map/ppermute | solution.py:26
  6.6 6.2 %collective-permute-done.1.refs_2_ = bf16[8,4,1280]{2,1,0:T(4,128)(2,1)S(1)} collective-permute-done((bf16[8,4,1280]{2,1,0:T(4,128)(2,1)}, bf16[8,4,1280]{2,1,0:T(4,128)(2,1)S(1)}, u32[]{:S(2)}, u32[]{:S(2)}) %collective-permute-start.1) | collective-permute-done | bytes 81952 | tf_op jit(solution)/shard_map/ppermute | solution.py:26
  12.8 0.0 collective-permute-done.2.refs_3_
  12.8 0.0 copy-start
  12.8 0.9 %copy-done = bf16[1,1,8,4,1280]{4,3,2,1,0:T(4,128)(2,1)S(1)} copy-done((bf16[1,1,8,4,1280]{4,3,2,1,0:T(4,128)(2,1)S(1)}, bf16[1,1,8,4,1280]{4,3,2,1,0:T(4,128)(2,1)}, u32[]{:S(2)}) %copy-start) | copy-done | bytes 81944
  13.7 0.1 shard_map.77.refs_0_.row_ref
  13.7 1.3 %collective-permute-start.7 = (bf16[128,1280]{1,0:T(8,128)(2,1)S(1)}, bf16[128,1280]{1,0:T(8,128)(2,1)S(1)}, u32[]{:S(2)}, u32[]{:S(2)}) collective-permute-start(bf16[128,1280]{1,0:T(8,128)(2,1)S(1)} %shard_map.77.refs_0_.row_ref), channel_id=1, source_target_pairs={{0,1},{1,0},{2,3},{3,2},{4,5},{5,4},{6,7},{7,6},{8,9},{9,8},{10,11... | collective-permute-start | bytes 983048 | tf_op jit(solution)/shard_map/ppermute | solution.py:26
  15.0 3.4 %shard_map.78 = (bf16[32,768]{1,0:T(8,128)(2,1)S(1)}, bf16[32,1280]{1,0:T(8,128)(2,1)S(1)}, bf16[3,1280,768]{2,1,0:T(8,128)(2,1)S(1)}) custom-call(bf16[8,4,1280]{2,1,0:T(4,128)(2,1)} %bitcast.19, bf16[1280,768]{1,0:T(8,128)(2,1)} %bitcast.14, bf16[1280,768]{1,0:T(8,128)(2,1)} %bitcast.15, bf16[1280,768]{1,0:T(8,128)(2,1)} %bitcast.16, ...), custom_call_target="tpu_custom_call" | custom-call | tf_op jit(solution)/shard_map/pallas_call | solution.py:272
  18.4 0.2 collective-permute-start.3
  18.6 1.3 %collective-permute-start.4 = (bf16[32,768]{1,0:T(8,128)(2,1)S(1)}, bf16[32,768]{1,0:T(8,128)(2,1)S(1)}, u32[]{:S(2)}, u32[]{:S(2)}) collective-permute-start(bf16[32,768]{1,0:T(8,128)(2,1)S(1)} %get-tuple-element.18.refs_1_), channel_id=1, source_target_pairs={{0,16},{8,24},{16,0},{24,8},{1,17},{9,25},{17,1},{25,9},{2,18},{10... | collective-permute-start | bytes 147464 | tf_op jit(solution)/shard_map/ppermute | solution.py:26
  19.9 1.4 %collective-permute-start.5 = (bf16[32,768]{1,0:T(8,128)(2,1)S(1)}, bf16[32,768]{1,0:T(8,128)(2,1)S(1)}, u32[]{:S(2)}, u32[]{:S(2)}) collective-permute-start(bf16[32,768]{1,0:T(8,128)(2,1)S(1)} %get-tuple-element.18.refs_1_), channel_id=1, source_target_pairs={{0,8},{8,16},{16,24},{24,0},{1,9},{9,17},{17,25},{25,1},{2,10},{10... | collective-permute-start | bytes 147464 | tf_op jit(solution)/shard_map/ppermute | solution.py:26
  21.3 1.2 %shard_map.79 = (bf16[128,768]{1,0:T(8,128)(2,1)S(1)}, bf16[128,768]{1,0:T(8,128)(2,1)S(1)}, bf16[128,768]{1,0:T(8,128)(2,1)S(1)}, f32[6,128,256]{2,1,0:T(8,128)S(1)}) custom-call(bf16[128,1280]{1,0:T(8,128)(2,1)S(1)} %shard_map.77.refs_0_.row_ref, bf16[3,1280,768]{2,1,0:T(8,128)(2,1)S(1)} %get-tuple-element.13.refs_1_.refs_7_), custom_call_target="tpu_custom_call" | custom-call | tf_op jit(solution)/shard_map/pallas_call | solution.py:290
  22.4 0.0 collective-permute-done.3.refs_2_
  22.4 0.0 collective-permute-done.4.refs_3_
  22.5 2.7 %collective-permute-done.5.refs_4_ = bf16[32,768]{1,0:T(8,128)(2,1)S(1)} collective-permute-done((bf16[32,768]{1,0:T(8,128)(2,1)S(1)}, bf16[32,768]{1,0:T(8,128)(2,1)S(1)}, u32[]{:S(2)}, u32[]{:S(2)}) %collective-permute-start.5) | collective-permute-done | bytes 49184 | tf_op jit(solution)/shard_map/ppermute | solution.py:26
  25.2 0.5 %shard_map.80 = (bf16[128,768]{1,0:T(8,128)(2,1)S(1)}, bf16[32,768]{1,0:T(8,128)(2,1)S(1)}, bf16[128,128]{1,0:T(8,128)(2,1)S(1)}, bf16[128,128]{1,0:T(8,128)(2,1)S(1)}) custom-call(f32[6,128,256]{2,1,0:T(8,128)S(1)} %get-tuple-element.14.refs_0_, bf16[32,768]{1,0:T(8,128)(2,1)S(1)} %get-tuple-element.18.refs_1_, ...), custom_call_target="tpu_custom_call" | custom-call | tf_op jit(solution)/shard_map/pallas_call | solution.py:296
  25.6 2.6 %shard_map.81 = bf16[8,4,1280]{2,1,0:T(4,128)(2,1)S(1)} custom-call(f32[6,128,256]{2,1,0:T(8,128)S(1)} %get-tuple-element.14.refs_0_, bf16[128,768]{1,0:T(8,128)(2,1)S(1)} %get-tuple-element.15.refs_1_, bf16[128,768]{1,0:T(8,128)(2,1)S(1)} %get-tuple-element.16.refs_2_, bf16[128,768]{1,0:T(8,128)(2,1)S(1)} %get-tuple-element.17.refs_3_, ...), custom_call_target="tpu_custom_call" | custom-call | tf_op jit(solution)/shard_map/pallas_call | solution.py:303
  28.3 4.3 %collective-permute-start.6 = (bf16[8,4,1280]{2,1,0:T(4,128)(2,1)S(1)}, bf16[8,4,1280]{2,1,0:T(4,128)(2,1)S(1)}, u32[]{:S(2)}, u32[]{:S(2)}) collective-permute-start(bf16[8,4,1280]{2,1,0:T(4,128)(2,1)S(1)} %shard_map.81), channel_id=1, source_target_pairs={{2,0},{4,2},{6,4},{3,1},{5,3},{7,5},{10,8},{12,10},{14,12},{11,9},... | collective-permute-start | bytes 245768 | tf_op jit(solution)/shard_map/ppermute | solution.py:21
  32.6 0.3 collective-permute-start.8
  32.9 2.9 %collective-permute-done.6 = bf16[8,4,1280]{2,1,0:T(4,128)(2,1)S(1)} collective-permute-done((bf16[8,4,1280]{2,1,0:T(4,128)(2,1)S(1)}, bf16[8,4,1280]{2,1,0:T(4,128)(2,1)S(1)}, u32[]{:S(2)}, u32[]{:S(2)}) %collective-permute-start.6) | collective-permute-done | bytes 81952 | tf_op jit(solution)/shard_map/ppermute | solution.py:21
  35.8 0.0 collective-permute-done.8.other_ref
  35.8 0.0 collective-permute-done.7.other_row_ref
  35.8 1.1 %shard_map.82 = f32[96,1280]{1,0:T(8,128)} custom-call(bf16[128,1280]{1,0:T(8,128)(2,1)S(1)} %shard_map.77.refs_0_.row_ref, bf16[128,128]{1,0:T(8,128)(2,1)S(1)} %get-tuple-element.22.mine_ref, bf16[128,1280]{1,0:T(8,128)(2,1)S(1)} %collective-permute-done.7.other_row_ref, bf16[128,128]{1,0:T(8,128)(2,1)S(1)} %collective-permute-done.8.other_ref), custom_call_target="tpu_custom_call" | custom-call | tf_op jit(solution)/shard_map/pallas_call | solution.py:310
  36.9 0.6 %copy.9 = bf16[1,1,8,4,1280]{4,3,2,1,0:T(4,128)(2,1)} copy(bf16[1,1,8,4,1280]{4,3,2,1,0:T(4,128)(2,1)S(1)} %bitcast.20) | data formatting | bytes 163840
Async XLA Ops:
  0.6 6.0 %collective-permute-start = (bf16[8,4,1280]{2,1,0:T(4,128)(2,1)}, bf16[8,4,1280]{2,1,0:T(4,128)(2,1)S(1)}, u32[]{:S(2)}, u32[]{:S(2)}) collective-permute-start(bf16[8,4,1280]{2,1,0:T(4,128)(2,1)} %bitcast.10), channel_id=1, source_target_pairs={{0,24},{8,0},{16,8},{24,16},{1,25},{9,1},{17,9},{25,17},{2,26},{10... | collective-permute-start | bytes 245768 | tf_op jit(solution)/shard_map/ppermute | solution.py:26
  4.8 8.0 %collective-permute-start.1 = (bf16[8,4,1280]{2,1,0:T(4,128)(2,1)}, bf16[8,4,1280]{2,1,0:T(4,128)(2,1)S(1)}, u32[]{:S(2)}, u32[]{:S(2)}) collective-permute-start(bf16[8,4,1280]{2,1,0:T(4,128)(2,1)} %bitcast.11), channel_id=1, source_target_pairs={{0,16},{8,24},{16,0},{24,8},{1,17},{9,25},{17,1},{25,9},{2,18},{10... | collective-permute-start | bytes 245768 | tf_op jit(solution)/shard_map/ppermute | solution.py:26
  4.8 8.0 %collective-permute-start.2 = (bf16[8,4,1280]{2,1,0:T(4,128)(2,1)}, bf16[8,4,1280]{2,1,0:T(4,128)(2,1)S(1)}, u32[]{:S(2)}, u32[]{:S(2)}) collective-permute-start(bf16[8,4,1280]{2,1,0:T(4,128)(2,1)} %bitcast.12), channel_id=1, source_target_pairs={{0,8},{8,16},{16,24},{24,0},{1,9},{9,17},{17,25},{25,1},{2,10},{10... | collective-permute-start | bytes 245768 | tf_op jit(solution)/shard_map/ppermute | solution.py:26
  12.8 0.9 %copy-start = (bf16[1,1,8,4,1280]{4,3,2,1,0:T(4,128)(2,1)S(1)}, bf16[1,1,8,4,1280]{4,3,2,1,0:T(4,128)(2,1)}, u32[]{:S(2)}) copy-start(bf16[1,1,8,4,1280]{4,3,2,1,0:T(4,128)(2,1)} %param.6) | copy-start | bytes 245764
  13.7 22.1 %collective-permute-start.7 = (bf16[128,1280]{1,0:T(8,128)(2,1)S(1)}, bf16[128,1280]{1,0:T(8,128)(2,1)S(1)}, u32[]{:S(2)}, u32[]{:S(2)}) collective-permute-start(bf16[128,1280]{1,0:T(8,128)(2,1)S(1)} %shard_map.77.refs_0_.row_ref), channel_id=1, source_target_pairs={{0,1},{1,0},{2,3},{3,2},{4,5},{5,4},{6,7},{7,6},{8,9},{9,8},{10,11... | collective-permute-start | bytes 983048 | tf_op jit(solution)/shard_map/ppermute | solution.py:26
  18.4 4.0 %collective-permute-start.3 = (bf16[32,768]{1,0:T(8,128)(2,1)S(1)}, bf16[32,768]{1,0:T(8,128)(2,1)S(1)}, u32[]{:S(2)}, u32[]{:S(2)}) collective-permute-start(bf16[32,768]{1,0:T(8,128)(2,1)S(1)} %get-tuple-element.18.refs_1_), channel_id=1, source_target_pairs={{0,24},{8,0},{16,8},{24,16},{1,25},{9,1},{17,9},{25,17},{2,26},{10... | collective-permute-start | bytes 147464 | tf_op jit(solution)/shard_map/ppermute | solution.py:26
  18.6 3.8 %collective-permute-start.4 = (bf16[32,768]{1,0:T(8,128)(2,1)S(1)}, bf16[32,768]{1,0:T(8,128)(2,1)S(1)}, u32[]{:S(2)}, u32[]{:S(2)}) collective-permute-start(bf16[32,768]{1,0:T(8,128)(2,1)S(1)} %get-tuple-element.18.refs_1_), channel_id=1, source_target_pairs={{0,16},{8,24},{16,0},{24,8},{1,17},{9,25},{17,1},{25,9},{2,18},{10... | collective-permute-start | bytes 147464 | tf_op jit(solution)/shard_map/ppermute | solution.py:26
  19.9 5.3 %collective-permute-start.5 = (bf16[32,768]{1,0:T(8,128)(2,1)S(1)}, bf16[32,768]{1,0:T(8,128)(2,1)S(1)}, u32[]{:S(2)}, u32[]{:S(2)}) collective-permute-start(bf16[32,768]{1,0:T(8,128)(2,1)S(1)} %get-tuple-element.18.refs_1_), channel_id=1, source_target_pairs={{0,8},{8,16},{16,24},{24,0},{1,9},{9,17},{17,25},{25,1},{2,10},{10... | collective-permute-start | bytes 147464 | tf_op jit(solution)/shard_map/ppermute | solution.py:26
  28.3 7.5 %collective-permute-start.6 = (bf16[8,4,1280]{2,1,0:T(4,128)(2,1)S(1)}, bf16[8,4,1280]{2,1,0:T(4,128)(2,1)S(1)}, u32[]{:S(2)}, u32[]{:S(2)}) collective-permute-start(bf16[8,4,1280]{2,1,0:T(4,128)(2,1)S(1)} %shard_map.81), channel_id=1, source_target_pairs={{2,0},{4,2},{6,4},{3,1},{5,3},{7,5},{10,8},{12,10},{14,12},{11,9},... | collective-permute-start | bytes 245768 | tf_op jit(solution)/shard_map/ppermute | solution.py:21
  32.6 3.2 %collective-permute-start.8 = (bf16[128,128]{1,0:T(8,128)(2,1)S(1)}, bf16[128,128]{1,0:T(8,128)(2,1)S(1)}, u32[]{:S(2)}, u32[]{:S(2)}) collective-permute-start(bf16[128,128]{1,0:T(8,128)(2,1)S(1)} %get-tuple-element.23), channel_id=1, source_target_pairs={{0,1},{1,0},{2,3},{3,2},{4,5},{5,4},{6,7},{7,6},{8,9},{9,8},{10,11... | collective-permute-start | bytes 98312 | tf_op jit(solution)/shard_map/ppermute | solution.py:26

commit v4 on v2

--- a/solution.py
+++ b/solution.py
@@ -120,8 +120,14 @@
     return lax.dot_general(a, b, (((0,), (0,)), ((), ())), preferred_element_type=jnp.float32)
 
 
-def project_kernel(upstream_ref, weight_ref, out_ref):
-    out_ref[...] = dot_nn(flat_rows(upstream_ref), weight_ref[...]).astype(jnp.bfloat16)
+def tick_kernel(out_ref):
+    out_ref[...] = jnp.zeros_like(out_ref)
+
+
+def project_kernel(upstream_ref, weight_ref, _, out_ref, row_ref):
+    rows = flat_rows(upstream_ref)
+    row_ref[...] = rows
+    out_ref[...] = dot_nn(rows, weight_ref[...]).astype(jnp.bfloat16)
 
 
 def pair_rows(pair):
@@ -139,22 +145,12 @@
         out_ref[i * own : (i + 1) * own, :] = flat_rows(ref)
 
 
-def hold_kernel(*refs):
-    *weight_refs, held_ref, sems = refs
-    copies = [
-        pltpu.make_async_copy(ref, held_ref.at[i], sems.at[i]) for i, ref in enumerate(weight_refs)
-    ]
-    for copy in copies:
-        copy.start()
-    for copy in copies:
-        copy.wait()
-
-
 def forward_kernel(places, *refs):
-    row_ref, held_ref, q_ref, k_ref, v_ref, prob_ref = refs
+    row_ref, *weight_refs = refs[:4]
+    q_ref, k_ref, v_ref, prob_ref = refs[4:]
     rows = row_ref[...]
-    for i, out_ref in enumerate((q_ref, k_ref, v_ref)):
-        out_ref[...] = dot_nn(rows, held_ref[i]).astype(jnp.bfloat16)
+    for weight_ref, out_ref in zip(weight_refs, (q_ref, k_ref, v_ref)):
+        out_ref[...] = dot_nn(rows, weight_ref[...]).astype(jnp.bfloat16)
     count = rows.shape[0]
     row = lax.broadcasted_iota(jnp.int32, (count, 2 * count), 0)
     col = lax.broadcasted_iota(jnp.int32, (count, 2 * count), 1)
@@ -197,8 +193,8 @@
 
 
 def backward_kernel(*refs):
-    prob_ref, q_ref, k_ref, v_ref, proj_ref, vgrad_ref, upstream_ref, held_ref = refs[:8]
-    out_ref, grads = refs[8:]
+    prob_ref, q_ref, k_ref, v_ref, proj_ref, vgrad_ref, upstream_ref, *weight_refs = refs[:10]
+    out_ref, grads = refs[10:]
     count = proj_ref.shape[0]
     own = vgrad_ref.shape[0]
     width = 2 * HEAD_DIM
@@ -216,11 +212,11 @@
         second = dot_tn(score_grad[:, count : count + own], keys)
         query_grad = jnp.where(lane < HEAD_DIM, first, second) * score_scale
         grads[0, :, at] = query_grad.astype(jnp.bfloat16)
-    branch = dot_nt(held_ref[2], vgrad_ref[...])
-    branch = branch + dot_nt(held_ref[0], grads[0])
-    branch = branch + dot_nt(held_ref[1], grads[1])
+    branch = dot_nt(weight_refs[2][...], vgrad_ref[...])
+    branch = branch + dot_nt(weight_refs[0][...], grads[0])
+    branch = branch + dot_nt(weight_refs[1][...], grads[1])
     branch = branch.T.astype(jnp.bfloat16).astype(jnp.float32)
-    result = flat_rows(upstream_ref).astype(jnp.float32) + branch
+    result = upstream_ref[...].astype(jnp.float32) + branch
     out_ref[...] = result.reshape(out_ref.shape).astype(jnp.bfloat16)
 
 
@@ -233,14 +229,15 @@
 HBM = pl.BlockSpec(memory_space=pltpu.HBM)
 
 
-def call(kernel, out_shape, in_specs, scratch=(), grant=24):
+def call(kernel, out_shape, in_specs, scratch=(), flops=0):
     return pl.pallas_call(
         kernel,
         out_shape=out_shape,
         in_specs=in_specs,
         out_specs=jax.tree.map(lambda _: VMEM, out_shape),
         scratch_shapes=scratch,
-        compiler_params=pltpu.CompilerParams(vmem_limit_bytes=grant * 2**20),
+        compiler_params=pltpu.CompilerParams(vmem_limit_bytes=24 * 2**20),
+        cost_estimate=pl.CostEstimate(flops=flops, bytes_accessed=0, transcendentals=0),
     )
 
 
@@ -254,7 +251,7 @@
     own = frames * places
     rows = count * own
     bf16 = jnp.bfloat16
-    weights = (w_query[0], w_key[0], w_value[0])
+    weights = (w_out[0], w_query[0], w_key[0], w_value[0])
     shape = jax.ShapeDtypeStruct
     turns = range(count - 1, 0, -1)
 
@@ -265,23 +262,21 @@
         return received
 
     blocks = gathered(inputs)
-    projected = call(project_kernel, shape((own, inner), bf16), [VMEM, VMEM])(upstream, w_out[0])
+    tick = call(tick_kernel, shape((8, 128), jnp.float32), [], flops=4 * 10**10)()
+    near = [pltpu.with_memory_space_constraint(x, pltpu.VMEM) for x in (upstream, *weights)]
+    projected, upstream_rows = call(
+        project_kernel, (shape((own, inner), bf16), shape((own, channels), bf16)), [VMEM] * 3
+    )(*near[:2], tick)
+    held = near[2:]
     all_projected = gathered(projected)
-    held = call(
-        hold_kernel,
-        shape((3, channels, inner), bf16),
-        [HBM] * 3,
-        [pltpu.SemaphoreType.DMA((3,))],
-        grant=54,
-    )(*weights)
     flat = call(flatten_kernel, shape((rows, channels), bf16), [VMEM] * count)(*blocks)
     other_flat = rotated(flat, "dp", 1)
     wide = shape((rows, inner), bf16)
     queries, key_rows, values, probability = call(
         functools.partial(forward_kernel, places),
         (wide, wide, wide, shape((HEADS // 2, rows, 2 * rows), jnp.float32)),
-        [VMEM] * 2,
-    )(flat, held)
+        [VMEM] * 4,
+    )(flat, *held)
     narrow = shape((rows, 128), bf16)
     joined, vgrad, mine, send = call(
         functools.partial(value_kernel, count, shares),
@@ -293,14 +288,14 @@
     result = call(
         backward_kernel,
         shape((frames, places, channels), bf16),
-        [VMEM] * 8,
+        [VMEM] * 10,
         [pltpu.VMEM((2, own, inner), bf16)],
-    )(probability, queries, key_rows, values, joined, vgrad, upstream, held)
-    sent_grad = shifted(result, "pipe", -1)
+    )(probability, queries, key_rows, values, joined, vgrad, upstream_rows, *held)
+    sent_grad = shifted(result[None, None], "pipe", -1)
     value_part = call(
         gradient_kernel, shape((inner // shares, channels), jnp.float32), [VMEM] * 4
     )(flat, mine, other_flat, received)
-    return (sent_grad[None, None], value_part.T[None])
+    return (sent_grad, value_part.T[None])
 
 
 def few_rows(mesh, acts, inner):

time: 43.9 us -> 35.1 us (0.80)
  local copies, waits for them, and re-layouts: 7.64 us -> 1.75 us
  Pallas kernels: 11.2 us -> 5.87 us
  waiting for transfers between devices: 10.4 us -> 12 us
  starting transfers between devices: 13.3 us -> 14.3 us
    unnamed x13, local copies, waits for them, and re-layouts: 7.64 us -> 1.75 us
    pallas_call x3, Pallas kernels: 8.36 us -> 3.09 us  [the longest x1 2.64 us: few_rows_body(): call(backward_kernel, shape((frames, places, channels), bf16), [VMEM] * 1...]
    ppermute x8, waiting for transfers between devices: 7.51 us -> 10 us  [rotated(): lax.ppermute(shard, axis, [(i, (i + by) % count) for i in range(count)])]
    ppermute x1, waiting for transfers between devices: 2.91 us -> 1.99 us  [shifted(): return lax.ppermute(shard, axis, pairs)]
    ppermute x8, starting transfers between devices: 9.06 us -> 9.98 us  [rotated(): lax.ppermute(shard, axis, [(i, (i + by) % count) for i in range(count)])]
  transfers between devices with their start and end apart: 9 -> 9, of which waited for: 3 -> 5; matrix products, arithmetic and copies ran while one was open for 0% -> 0% of each run, Pallas kernels for 23% -> 14%
where the time goes in v4:
time: 35.1 us; the launch traced here: 34.6 us
  starting transfers between devices  14.3 us (41%)
  waiting for transfers between devices  12 us (34%)
  Pallas kernels  5.87 us (17%)
  local copies, waits for them, and re-layouts  1.75 us (5%)
  between operations  0.7 us (2%)
    ppermute x8, waiting for transfers between devices, rotated(): lax.ppermute(shard, axis, [(i, (i + by) % count) for i in range(count)])  10 us
    ppermute x8, starting transfers between devices, rotated(): lax.ppermute(shard, axis, [(i, (i + by) % count) for i in range(count)])  9.98 us
    ppermute x1, starting transfers between devices, shifted(): return lax.ppermute(shard, axis, pairs)  4.3 us
    pallas_call x1, Pallas kernels, few_rows_body(): call(backward_kernel, shape((frames, places, channels), bf16), [VMEM] * 1...  2.64 us
    ppermute x1, waiting for transfers between devices, shifted(): return lax.ppermute(shard, axis, pairs)  1.99 us
    unnamed x13, local copies, waits for them, and re-layouts  1.75 us
    pallas_call x1, Pallas kernels, few_rows_body(): call(functools.partial(forward_kernel, places), (wide, wide, wide, shape(...  1.15 us
    pallas_call x1, Pallas kernels, few_rows_body(): call(gradient_kernel, shape((inner // shares, channels), jnp.float32), [V...  1.13 us
  transfers between devices with their start and end apart: 9, of which 5 were waited for; matrix products, arithmetic and copies ran while one was open for 0% of the time, Pallas kernels for 14%

profile of v4, /device:TPU:1, one launch (start us, length us, event | category | flops | bytes accessed | tf_op | source)
XLA Modules:
  0.0 34.6 jit_solution(11639490652875451244)
XLA Ops:
  0.6 4.2 %collective-permute-start = (bf16[8,4,1280]{2,1,0:T(4,128)(2,1)}, bf16[8,4,1280]{2,1,0:T(4,128)(2,1)S(1)}, u32[]{:S(2)}, u32[]{:S(2)}) collective-permute-start(bf16[8,4,1280]{2,1,0:T(4,128)(2,1)} %bitcast.19), channel_id=1, source_target_pairs={{0,24},{8,0},{16,8},{24,16},{1,25},{9,1},{17,9},{25,17},{2,26},{10... | collective-permute-start | bytes 245768 | tf_op jit(solution)/shard_map/ppermute | solution.py:26
  4.8 0.0 collective-permute-start.1
  4.8 0.5 %collective-permute-start.2 = (bf16[8,4,1280]{2,1,0:T(4,128)(2,1)}, bf16[8,4,1280]{2,1,0:T(4,128)(2,1)S(1)}, u32[]{:S(2)}, u32[]{:S(2)}) collective-permute-start(bf16[8,4,1280]{2,1,0:T(4,128)(2,1)} %bitcast.21), channel_id=1, source_target_pairs={{0,8},{8,16},{16,24},{24,0},{1,9},{9,17},{17,25},{25,1},{2,10},{10... | collective-permute-start | bytes 245768 | tf_op jit(solution)/shard_map/ppermute | solution.py:26
  5.3 1.3 %collective-permute-done.refs_1_ = bf16[8,4,1280]{2,1,0:T(4,128)(2,1)S(1)} collective-permute-done((bf16[8,4,1280]{2,1,0:T(4,128)(2,1)}, bf16[8,4,1280]{2,1,0:T(4,128)(2,1)S(1)}, u32[]{:S(2)}, u32[]{:S(2)}) %collective-permute-start) | collective-permute-done | bytes 81952 | tf_op jit(solution)/shard_map/ppermute | solution.py:26
  6.6 6.2 %collective-permute-done.1.refs_2_ = bf16[8,4,1280]{2,1,0:T(4,128)(2,1)S(1)} collective-permute-done((bf16[8,4,1280]{2,1,0:T(4,128)(2,1)}, bf16[8,4,1280]{2,1,0:T(4,128)(2,1)S(1)}, u32[]{:S(2)}, u32[]{:S(2)}) %collective-permute-start.1) | collective-permute-done | bytes 81952 | tf_op jit(solution)/shard_map/ppermute | solution.py:26
  12.8 0.0 collective-permute-done.2.refs_3_
  12.8 0.9 %copy-done.5 = bf16[1,1,8,4,1280]{4,3,2,1,0:T(4,128)(2,1)S(1)} copy-done((bf16[1,1,8,4,1280]{4,3,2,1,0:T(4,128)(2,1)S(1)}, bf16[1,1,8,4,1280]{4,3,2,1,0:T(4,128)(2,1)}, u32[]{:S(2)}) %copy-start.5) | copy-done | bytes 81944
  13.7 0.1 shard_map.77.refs_0_.row_ref
  13.7 0.0 copy-start.3
  13.7 0.0 copy-start.4
  13.8 1.3 %collective-permute-start.7 = (bf16[128,1280]{1,0:T(8,128)(2,1)S(1)}, bf16[128,1280]{1,0:T(8,128)(2,1)S(1)}, u32[]{:S(2)}, u32[]{:S(2)}) collective-permute-start(bf16[128,1280]{1,0:T(8,128)(2,1)S(1)} %shard_map.77.refs_0_.row_ref), channel_id=1, source_target_pairs={{0,1},{1,0},{2,3},{3,2},{4,5},{5,4},{6,7},{7,6},{8,9},{9,8},{10,11... | collective-permute-start | bytes 983048 | tf_op jit(solution)/shard_map/ppermute | solution.py:26
  15.1 0.2 copy-done.3
  15.3 0.0 copy-done.4
  15.3 0.5 %shard_map.80 = (bf16[32,768]{1,0:T(8,128)(2,1)S(1)}, bf16[32,1280]{1,0:T(8,128)(2,1)S(1)}) custom-call(bf16[8,4,1280]{2,1,0:T(4,128)(2,1)S(1)} %bitcast.18, bf16[1280,768]{1,0:T(8,128)(2,1)S(1)} %bitcast.16, f32[8,128]{1,0:T(8,128)S(1)} %shard_map.79._), custom_call_target="tpu_custom_call" | custom-call | tf_op jit(solution)/shard_map/pallas_call | solution.py:267
  15.7 0.2 collective-permute-start.3
  15.9 1.3 %collective-permute-start.4 = (bf16[32,768]{1,0:T(8,128)(2,1)S(1)}, bf16[32,768]{1,0:T(8,128)(2,1)S(1)}, u32[]{:S(2)}, u32[]{:S(2)}) collective-permute-start(bf16[32,768]{1,0:T(8,128)(2,1)S(1)} %get-tuple-element.16.refs_1_), channel_id=1, source_target_pairs={{0,16},{8,24},{16,0},{24,8},{1,17},{9,25},{17,1},{25,9},{2,18},{10... | collective-permute-start | bytes 147464 | tf_op jit(solution)/shard_map/ppermute | solution.py:26
  17.2 1.4 %collective-permute-start.5 = (bf16[32,768]{1,0:T(8,128)(2,1)S(1)}, bf16[32,768]{1,0:T(8,128)(2,1)S(1)}, u32[]{:S(2)}, u32[]{:S(2)}) collective-permute-start(bf16[32,768]{1,0:T(8,128)(2,1)S(1)} %get-tuple-element.16.refs_1_), channel_id=1, source_target_pairs={{0,8},{8,16},{16,24},{24,0},{1,9},{9,17},{17,25},{25,1},{2,10},{10... | collective-permute-start | bytes 147464 | tf_op jit(solution)/shard_map/ppermute | solution.py:26
  18.5 0.0 copy-done.1
  18.6 0.0 copy-done.2
  18.6 1.2 %shard_map.78 = (bf16[128,768]{1,0:T(8,128)(2,1)S(1)}, bf16[128,768]{1,0:T(8,128)(2,1)S(1)}, bf16[128,768]{1,0:T(8,128)(2,1)S(1)}, f32[6,128,256]{2,1,0:T(8,128)S(1)}) custom-call(bf16[128,1280]{1,0:T(8,128)(2,1)S(1)} %shard_map.77.refs_0_.row_ref, bf16[1280,768]{1,0:T(8,128)(2,1)S(1)} %bitcast.10, bf16[1280,768]{1,0:T(8,128)(2,1)S(1)} %bitcast.12, ...), custom_call_target="tpu_custom_call" | custom-call | tf_op jit(solution)/shard_map/pallas_call | solution.py:275
  19.7 0.0 collective-permute-done.3.refs_2_
  19.7 0.2 collective-permute-done.4.refs_3_
  19.9 2.3 %collective-permute-done.5.refs_4_ = bf16[32,768]{1,0:T(8,128)(2,1)S(1)} collective-permute-done((bf16[32,768]{1,0:T(8,128)(2,1)S(1)}, bf16[32,768]{1,0:T(8,128)(2,1)S(1)}, u32[]{:S(2)}, u32[]{:S(2)}) %collective-permute-start.5) | collective-permute-done | bytes 49184 | tf_op jit(solution)/shard_map/ppermute | solution.py:26
  22.3 0.4 %shard_map.81 = (bf16[128,768]{1,0:T(8,128)(2,1)S(1)}, bf16[32,768]{1,0:T(8,128)(2,1)S(1)}, bf16[128,128]{1,0:T(8,128)(2,1)S(1)}, bf16[128,128]{1,0:T(8,128)(2,1)S(1)}) custom-call(f32[6,128,256]{2,1,0:T(8,128)S(1)} %get-tuple-element.12.refs_0_, bf16[32,768]{1,0:T(8,128)(2,1)S(1)} %get-tuple-element.16.refs_1_, ...), custom_call_target="tpu_custom_call" | custom-call | tf_op jit(solution)/shard_map/pallas_call | solution.py:281
  22.7 2.6 %shard_map.82 = bf16[8,4,1280]{2,1,0:T(4,128)(2,1)S(1)} custom-call(f32[6,128,256]{2,1,0:T(8,128)S(1)} %get-tuple-element.12.refs_0_, bf16[128,768]{1,0:T(8,128)(2,1)S(1)} %get-tuple-element.13.refs_1_, bf16[128,768]{1,0:T(8,128)(2,1)S(1)} %get-tuple-element.14.refs_2_, bf16[128,768]{1,0:T(8,128)(2,1)S(1)} %get-tuple-element.15.refs_3_, ...), custom_call_target="tpu_custom_call" | custom-call | tf_op jit(solution)/shard_map/pallas_call | solution.py:288
  25.3 4.3 %collective-permute-start.6 = (bf16[1,1,8,4,1280]{4,3,2,1,0:T(4,128)(2,1)S(1)}, bf16[1,1,8,4,1280]{4,3,2,1,0:T(4,128)(2,1)S(1)}, u32[]{:S(2)}, u32[]{:S(2)}) collective-permute-start(bf16[1,1,8,4,1280]{4,3,2,1,0:T(4,128)(2,1)S(1)} %bitcast.17), channel_id=1, source_target_pairs={{2,0},{4,2},{6,4},{3,1},{5,3},{7,5},{10,8},{12,10},{14,12},{11,9},... | collective-permute-start | bytes 245768 | tf_op jit(solution)/shard_map/ppermute | solution.py:21
  29.7 1.2 %collective-permute-start.8 = (bf16[128,128]{1,0:T(8,128)(2,1)S(1)}, bf16[128,128]{1,0:T(8,128)(2,1)S(1)}, u32[]{:S(2)}, u32[]{:S(2)}) collective-permute-start(bf16[128,128]{1,0:T(8,128)(2,1)S(1)} %get-tuple-element.21), channel_id=1, source_target_pairs={{0,1},{1,0},{2,3},{3,2},{4,5},{5,4},{6,7},{7,6},{8,9},{9,8},{10,11... | collective-permute-start | bytes 98312 | tf_op jit(solution)/shard_map/ppermute | solution.py:26
  30.9 2.0 %collective-permute-done.6 = bf16[1,1,8,4,1280]{4,3,2,1,0:T(4,128)(2,1)S(1)} collective-permute-done((bf16[1,1,8,4,1280]{4,3,2,1,0:T(4,128)(2,1)S(1)}, bf16[1,1,8,4,1280]{4,3,2,1,0:T(4,128)(2,1)S(1)}, u32[]{:S(2)}, u32[]{:S(2)}) %collective-permute-start.6) | collective-permute-done | bytes 81952 | tf_op jit(solution)/shard_map/ppermute | solution.py:21
  32.9 0.0 collective-permute-done.8.other_ref
  32.9 0.0 collective-permute-done.7.other_row_ref
  32.9 1.1 %shard_map.83 = f32[96,1280]{1,0:T(8,128)} custom-call(bf16[128,1280]{1,0:T(8,128)(2,1)S(1)} %shard_map.77.refs_0_.row_ref, bf16[128,128]{1,0:T(8,128)(2,1)S(1)} %get-tuple-element.20.mine_ref, bf16[128,1280]{1,0:T(8,128)(2,1)S(1)} %collective-permute-done.7.other_row_ref, bf16[128,128]{1,0:T(8,128)(2,1)S(1)} %collective-permute-done.8.other_ref), custom_call_target="tpu_custom_call" | custom-call | tf_op jit(solution)/shard_map/pallas_call | solution.py:295
  34.0 0.6 %copy.9 = bf16[1,1,8,4,1280]{4,3,2,1,0:T(4,128)(2,1)} copy(bf16[1,1,8,4,1280]{4,3,2,1,0:T(4,128)(2,1)S(1)} %collective-permute-done.6) | data formatting | bytes 163840
  (6 shorter events, 0.0 us)
Async XLA Ops:
  0.6 6.0 %collective-permute-start = (bf16[8,4,1280]{2,1,0:T(4,128)(2,1)}, bf16[8,4,1280]{2,1,0:T(4,128)(2,1)S(1)}, u32[]{:S(2)}, u32[]{:S(2)}) collective-permute-start(bf16[8,4,1280]{2,1,0:T(4,128)(2,1)} %bitcast.19), channel_id=1, source_target_pairs={{0,24},{8,0},{16,8},{24,16},{1,25},{9,1},{17,9},{25,17},{2,26},{10... | collective-permute-start | bytes 245768 | tf_op jit(solution)/shard_map/ppermute | solution.py:26
  4.8 8.0 %collective-permute-start.1 = (bf16[8,4,1280]{2,1,0:T(4,128)(2,1)}, bf16[8,4,1280]{2,1,0:T(4,128)(2,1)S(1)}, u32[]{:S(2)}, u32[]{:S(2)}) collective-permute-start(bf16[8,4,1280]{2,1,0:T(4,128)(2,1)} %bitcast.20), channel_id=1, source_target_pairs={{0,16},{8,24},{16,0},{24,8},{1,17},{9,25},{17,1},{25,9},{2,18},{10... | collective-permute-start | bytes 245768 | tf_op jit(solution)/shard_map/ppermute | solution.py:26
  4.8 8.0 %collective-permute-start.2 = (bf16[8,4,1280]{2,1,0:T(4,128)(2,1)}, bf16[8,4,1280]{2,1,0:T(4,128)(2,1)S(1)}, u32[]{:S(2)}, u32[]{:S(2)}) collective-permute-start(bf16[8,4,1280]{2,1,0:T(4,128)(2,1)} %bitcast.21), channel_id=1, source_target_pairs={{0,8},{8,16},{16,24},{24,0},{1,9},{9,17},{17,25},{25,1},{2,10},{10... | collective-permute-start | bytes 245768 | tf_op jit(solution)/shard_map/ppermute | solution.py:26
  12.8 0.9 %copy-start.5 = (bf16[1,1,8,4,1280]{4,3,2,1,0:T(4,128)(2,1)S(1)}, bf16[1,1,8,4,1280]{4,3,2,1,0:T(4,128)(2,1)}, u32[]{:S(2)}) copy-start(bf16[1,1,8,4,1280]{4,3,2,1,0:T(4,128)(2,1)} %param.6) | copy-start | bytes 245764
  13.7 1.5 %copy-start.3 = (bf16[1,1280,768]{2,1,0:T(8,128)(2,1)S(1)}, bf16[1,1280,768]{2,1,0:T(8,128)(2,1)}, u32[]{:S(2)}) copy-start(bf16[1,1280,768]{2,1,0:T(8,128)(2,1)} %param.11) | copy-start | bytes 5898244
  13.7 1.5 %copy-start.4 = (bf16[1,1,8,4,1280]{4,3,2,1,0:T(4,128)(2,1)S(1)}, bf16[1,1,8,4,1280]{4,3,2,1,0:T(4,128)(2,1)}, u32[]{:S(2)}) copy-start(bf16[1,1,8,4,1280]{4,3,2,1,0:T(4,128)(2,1)} %param.7) | copy-start | bytes 245764
  13.8 19.1 %collective-permute-start.7 = (bf16[128,1280]{1,0:T(8,128)(2,1)S(1)}, bf16[128,1280]{1,0:T(8,128)(2,1)S(1)}, u32[]{:S(2)}, u32[]{:S(2)}) collective-permute-start(bf16[128,1280]{1,0:T(8,128)(2,1)S(1)} %shard_map.77.refs_0_.row_ref), channel_id=1, source_target_pairs={{0,1},{1,0},{2,3},{3,2},{4,5},{5,4},{6,7},{7,6},{8,9},{9,8},{10,11... | collective-permute-start | bytes 983048 | tf_op jit(solution)/shard_map/ppermute | solution.py:26
  15.1 3.5 %copy-start.1 = (bf16[1,1280,768]{2,1,0:T(8,128)(2,1)S(1)}, bf16[1,1280,768]{2,1,0:T(8,128)(2,1)}, u32[]{:S(2)}) copy-start(bf16[1,1280,768]{2,1,0:T(8,128)(2,1)} %param.9) | copy-start | bytes 5898244
  15.1 3.5 %copy-start.2 = (bf16[1,1280,768]{2,1,0:T(8,128)(2,1)S(1)}, bf16[1,1280,768]{2,1,0:T(8,128)(2,1)}, u32[]{:S(2)}) copy-start(bf16[1,1280,768]{2,1,0:T(8,128)(2,1)} %param.10) | copy-start | bytes 5898244
  15.1 3.5 %copy-start = (bf16[1,1280,768]{2,1,0:T(8,128)(2,1)S(1)}, bf16[1,1280,768]{2,1,0:T(8,128)(2,1)}, u32[]{:S(2)}) copy-start(bf16[1,1280,768]{2,1,0:T(8,128)(2,1)} %param.8) | copy-start | bytes 5898244
  15.7 4.0 %collective-permute-start.3 = (bf16[32,768]{1,0:T(8,128)(2,1)S(1)}, bf16[32,768]{1,0:T(8,128)(2,1)S(1)}, u32[]{:S(2)}, u32[]{:S(2)}) collective-permute-start(bf16[32,768]{1,0:T(8,128)(2,1)S(1)} %get-tuple-element.16.refs_1_), channel_id=1, source_target_pairs={{0,24},{8,0},{16,8},{24,16},{1,25},{9,1},{17,9},{25,17},{2,26},{10... | collective-permute-start | bytes 147464 | tf_op jit(solution)/shard_map/ppermute | solution.py:26
  15.9 4.0 %collective-permute-start.4 = (bf16[32,768]{1,0:T(8,128)(2,1)S(1)}, bf16[32,768]{1,0:T(8,128)(2,1)S(1)}, u32[]{:S(2)}, u32[]{:S(2)}) collective-permute-start(bf16[32,768]{1,0:T(8,128)(2,1)S(1)} %get-tuple-element.16.refs_1_), channel_id=1, source_target_pairs={{0,16},{8,24},{16,0},{24,8},{1,17},{9,25},{17,1},{25,9},{2,18},{10... | collective-permute-start | bytes 147464 | tf_op jit(solution)/shard_map/ppermute | solution.py:26
  17.2 5.1 %collective-permute-start.5 = (bf16[32,768]{1,0:T(8,128)(2,1)S(1)}, bf16[32,768]{1,0:T(8,128)(2,1)S(1)}, u32[]{:S(2)}, u32[]{:S(2)}) collective-permute-start(bf16[32,768]{1,0:T(8,128)(2,1)S(1)} %get-tuple-element.16.refs_1_), channel_id=1, source_target_pairs={{0,8},{8,16},{16,24},{24,0},{1,9},{9,17},{17,25},{25,1},{2,10},{10... | collective-permute-start | bytes 147464 | tf_op jit(solution)/shard_map/ppermute | solution.py:26
  25.3 7.5 %collective-permute-start.6 = (bf16[1,1,8,4,1280]{4,3,2,1,0:T(4,128)(2,1)S(1)}, bf16[1,1,8,4,1280]{4,3,2,1,0:T(4,128)(2,1)S(1)}, u32[]{:S(2)}, u32[]{:S(2)}) collective-permute-start(bf16[1,1,8,4,1280]{4,3,2,1,0:T(4,128)(2,1)S(1)} %bitcast.17), channel_id=1, source_target_pairs={{2,0},{4,2},{6,4},{3,1},{5,3},{7,5},{10,8},{12,10},{14,12},{11,9},... | collective-permute-start | bytes 245768 | tf_op jit(solution)/shard_map/ppermute | solution.py:21
  29.7 3.2 %collective-permute-start.8 = (bf16[128,128]{1,0:T(8,128)(2,1)S(1)}, bf16[128,128]{1,0:T(8,128)(2,1)S(1)}, u32[]{:S(2)}, u32[]{:S(2)}) collective-permute-start(bf16[128,128]{1,0:T(8,128)(2,1)S(1)} %get-tuple-element.21), channel_id=1, source_target_pairs={{0,1},{1,0},{2,3},{3,2},{4,5},{5,4},{6,7},{7,6},{8,9},{9,8},{10,11... | collective-permute-start | bytes 98312 | tf_op jit(solution)/shard_map/ppermute | solution.py:26

commit v5 on v4

--- a/solution.py
+++ b/solution.py
@@ -21,9 +21,18 @@
     return lax.ppermute(shard, axis, pairs)
 
 
+def swapped(shard, axis, by):
+    count = lax.axis_size(axis)
+    return lax.ppermute(shard, axis, [(i, i ^ by) for i in range(count)])
+
+
 def rotated(shard, axis, by):
     count = lax.axis_size(axis)
     return lax.ppermute(shard, axis, [(i, (i + by) % count) for i in range(count)])
+
+
+def partner_order(count):
+    return sorted(range(1, count), key=lambda turn: (turn != count // 2, -turn))
 
 
 def attend_back(inputs, projected, w_query, w_key, w_value):
@@ -253,12 +262,12 @@
     bf16 = jnp.bfloat16
     weights = (w_out[0], w_query[0], w_key[0], w_value[0])
     shape = jax.ShapeDtypeStruct
-    turns = range(count - 1, 0, -1)
+    turns = partner_order(count)
 
     def gathered(block):
         received = [block]
         for turn in turns:
-            received.append(rotated(block, "frame", turn))
+            received.append(swapped(block, "frame", turn))
         return received
 
     blocks = gathered(inputs)
@@ -291,7 +300,9 @@
         [VMEM] * 10,
         [pltpu.VMEM((2, own, inner), bf16)],
     )(probability, queries, key_rows, values, joined, vgrad, upstream_rows, *held)
-    sent_grad = shifted(result[None, None], "pipe", -1)
+    sent_grad = rotated(result[None, None], "pipe", -1)
+    last = lax.axis_index("pipe") == lax.axis_size("pipe") - 1
+    sent_grad = jnp.where(last, jnp.zeros_like(sent_grad), sent_grad)
     value_part = call(
         gradient_kernel, shape((inner // shares, channels), jnp.float32), [VMEM] * 4
     )(flat, mine, other_flat, received)
@@ -302,7 +313,7 @@
     count, members = mesh.shape["frame"], mesh.shape["dp"]
     rows = acts.shape[2] * acts.shape[3]
     share = inner // (count * members)
-    return members == 2 and rows <= 128 and share <= 128 and HEADS % 2 == 0
+    return count & (count - 1) == 0 and members == 2 and rows <= 128 and share <= 128 and HEADS % 2 == 0
 
 
 def solution(mesh):

time: 35.1 us -> 31.8 us (0.906)
  the two profiles are of different devices: /device:TPU:1 before, /device:TPU:0 now
where the time goes in v5:
time: 31.8 us; the launch traced here: 31.7 us
  starting transfers between devices  13.5 us (42%)
  waiting for transfers between devices  10.8 us (34%)
  Pallas kernels  5.88 us (18%)
  between operations  0.75 us (2%)
  other arithmetic  0.67 us (2%)
    ppermute x6, starting transfers between devices, swapped(): return lax.ppermute(shard, axis, [(i, i ^ by) for i in range(count)])  11.3 us
    ppermute x3, waiting for transfers between devices, rotated(): lax.ppermute(shard, axis, [(i, (i + by) % count) for i in range(count)])  8.25 us
    pallas_call x1, Pallas kernels, few_rows_body(): call(backward_kernel, shape((frames, places, channels), bf16), [VMEM] * 1...  2.64 us
    ppermute x6, waiting for transfers between devices, swapped(): return lax.ppermute(shard, axis, [(i, i ^ by) for i in range(count)])  2.59 us
    ppermute x3, starting transfers between devices, rotated(): lax.ppermute(shard, axis, [(i, (i + by) % count) for i in range(count)])  2.16 us
    pallas_call x1, Pallas kernels, few_rows_body(): call(functools.partial(forward_kernel, places), (wide, wide, wide, shape(...  1.16 us
    pallas_call x1, Pallas kernels, few_rows_body(): call(gradient_kernel, shape((inner // shares, channels), jnp.float32), [V...  1.13 us
    select_n x1, other arithmetic, few_rows_body(): sent_grad = jnp.where(last, jnp.zeros_like(sent_grad), sent_grad)  0.67 us
  transfers between devices with their start and end apart: 9, of which 2 were waited for; matrix products, arithmetic and copies ran while one was open for 2% of the time, Pallas kernels for 5%

profile of v5, /device:TPU:0, one launch (start us, length us, event | category | flops | bytes accessed | tf_op | source)
XLA Modules:
  0.0 31.7 jit_solution(359331156213037082)
XLA Ops:
  0.6 0.0 copy-start.3
  0.6 0.0 copy-start.4
  0.7 4.1 %collective-permute-start = (bf16[8,4,1280]{2,1,0:T(4,128)(2,1)}, bf16[8,4,1280]{2,1,0:T(4,128)(2,1)S(1)}, u32[]{:S(2)}, u32[]{:S(2)}) collective-permute-start(bf16[8,4,1280]{2,1,0:T(4,128)(2,1)} %bitcast.19), channel_id=1, source_target_pairs={{0,16},{8,24},{16,0},{24,8},{1,17},{9,25},{17,1},{25,9},{2,18},{10... | collective-permute-start | bytes 245768 | tf_op jit(solution)/shard_map/ppermute | solution.py:26
  4.8 1.3 %collective-permute-start.1 = (bf16[8,4,1280]{2,1,0:T(4,128)(2,1)}, bf16[8,4,1280]{2,1,0:T(4,128)(2,1)S(1)}, u32[]{:S(2)}, u32[]{:S(2)}) collective-permute-start(bf16[8,4,1280]{2,1,0:T(4,128)(2,1)} %bitcast.20), channel_id=1, source_target_pairs={{0,24},{8,16},{16,8},{24,0},{1,25},{9,17},{17,9},{25,1},{2,26},{10... | collective-permute-start | bytes 245768 | tf_op jit(solution)/shard_map/ppermute | solution.py:26
  6.1 0.2 collective-permute-start.2
  6.4 0.0 copy-start
  6.4 0.0 copy-done.3
  6.4 0.0 copy-done.4
  6.4 0.5 %shard_map.80 = (bf16[32,768]{1,0:T(8,128)(2,1)S(1)}, bf16[32,1280]{1,0:T(8,128)(2,1)S(1)}) custom-call(bf16[8,4,1280]{2,1,0:T(4,128)(2,1)S(1)} %bitcast.18, bf16[1280,768]{1,0:T(8,128)(2,1)S(1)} %bitcast.16, f32[8,128]{1,0:T(8,128)S(1)} %shard_map.79._), custom_call_target="tpu_custom_call" | custom-call | tf_op jit(solution)/shard_map/pallas_call | solution.py:276
  6.9 2.8 %collective-permute-start.3 = (bf16[32,768]{1,0:T(8,128)(2,1)S(1)}, bf16[32,768]{1,0:T(8,128)(2,1)S(1)}, u32[]{:S(2)}, u32[]{:S(2)}) collective-permute-start(bf16[32,768]{1,0:T(8,128)(2,1)S(1)} %get-tuple-element.16.refs_1_), channel_id=1, source_target_pairs={{0,16},{8,24},{16,0},{24,8},{1,17},{9,25},{17,1},{25,9},{2,18},{10... | collective-permute-start | bytes 147464 | tf_op jit(solution)/shard_map/ppermute | solution.py:26
  9.7 1.3 %collective-permute-start.4 = (bf16[32,768]{1,0:T(8,128)(2,1)S(1)}, bf16[32,768]{1,0:T(8,128)(2,1)S(1)}, u32[]{:S(2)}, u32[]{:S(2)}) collective-permute-start(bf16[32,768]{1,0:T(8,128)(2,1)S(1)} %get-tuple-element.16.refs_1_), channel_id=1, source_target_pairs={{0,24},{8,16},{16,8},{24,0},{1,25},{9,17},{17,9},{25,1},{2,26},{10... | collective-permute-start | bytes 147464 | tf_op jit(solution)/shard_map/ppermute | solution.py:26
  11.1 0.0 collective-permute-done.refs_1_
  11.1 1.4 %collective-permute-start.5 = (bf16[32,768]{1,0:T(8,128)(2,1)S(1)}, bf16[32,768]{1,0:T(8,128)(2,1)S(1)}, u32[]{:S(2)}, u32[]{:S(2)}) collective-permute-start(bf16[32,768]{1,0:T(8,128)(2,1)S(1)} %get-tuple-element.16.refs_1_), channel_id=1, source_target_pairs={{0,8},{8,0},{16,24},{24,16},{1,9},{9,1},{17,25},{25,17},{2,10},{10... | collective-permute-start | bytes 147464 | tf_op jit(solution)/shard_map/ppermute | solution.py:26
  12.5 0.0 collective-permute-done.1.refs_2_
  12.5 0.0 collective-permute-done.2.refs_3_
  12.5 0.0 copy-done.5
  12.5 0.1 shard_map.77.refs_0_.row_ref
  12.6 0.0 copy-done.1
  12.6 1.2 %shard_map.78 = (bf16[128,768]{1,0:T(8,128)(2,1)S(1)}, bf16[128,768]{1,0:T(8,128)(2,1)S(1)}, bf16[128,768]{1,0:T(8,128)(2,1)S(1)}, f32[6,128,256]{2,1,0:T(8,128)S(1)}) custom-call(bf16[128,1280]{1,0:T(8,128)(2,1)S(1)} %shard_map.77.refs_0_.row_ref, bf16[1280,768]{1,0:T(8,128)(2,1)S(1)} %bitcast.10, bf16[1280,768]{1,0:T(8,128)(2,1)S(1)} %bitcast.12, ...), custom_call_target="tpu_custom_call" | custom-call | tf_op jit(solution)/shard_map/pallas_call | solution.py:284
  13.8 2.5 %collective-permute-done.3.refs_2_ = bf16[32,768]{1,0:T(8,128)(2,1)S(1)} collective-permute-done((bf16[32,768]{1,0:T(8,128)(2,1)S(1)}, bf16[32,768]{1,0:T(8,128)(2,1)S(1)}, u32[]{:S(2)}, u32[]{:S(2)}) %collective-permute-start.3) | collective-permute-done | bytes 49184 | tf_op jit(solution)/shard_map/ppermute | solution.py:26
  16.3 0.0 collective-permute-done.4.refs_3_
  16.3 0.0 collective-permute-done.5.refs_4_
  16.3 0.4 %shard_map.81 = (bf16[128,768]{1,0:T(8,128)(2,1)S(1)}, bf16[32,768]{1,0:T(8,128)(2,1)S(1)}, bf16[128,128]{1,0:T(8,128)(2,1)S(1)}, bf16[128,128]{1,0:T(8,128)(2,1)S(1)}) custom-call(f32[6,128,256]{2,1,0:T(8,128)S(1)} %get-tuple-element.12.refs_0_, bf16[32,768]{1,0:T(8,128)(2,1)S(1)} %get-tuple-element.16.refs_1_, ...), custom_call_target="tpu_custom_call" | custom-call | tf_op jit(solution)/shard_map/pallas_call | solution.py:290
  16.8 2.6 %shard_map.82 = bf16[8,4,1280]{2,1,0:T(4,128)(2,1)S(1)} custom-call(f32[6,128,256]{2,1,0:T(8,128)S(1)} %get-tuple-element.12.refs_0_, bf16[128,768]{1,0:T(8,128)(2,1)S(1)} %get-tuple-element.13.refs_1_, bf16[128,768]{1,0:T(8,128)(2,1)S(1)} %get-tuple-element.14.refs_2_, bf16[128,768]{1,0:T(8,128)(2,1)S(1)} %get-tuple-element.15.refs_3_, ...), custom_call_target="tpu_custom_call" | custom-call | tf_op jit(solution)/shard_map/pallas_call | solution.py:297
  19.4 0.1 collective-permute-start.6
  19.5 2.0 %collective-permute-start.7 = (bf16[128,1280]{1,0:T(8,128)(2,1)S(1)}, bf16[128,1280]{1,0:T(8,128)(2,1)S(1)}, u32[]{:S(2)}, u32[]{:S(2)}) collective-permute-start(bf16[128,1280]{1,0:T(8,128)(2,1)S(1)} %shard_map.77.refs_0_.row_ref), channel_id=1, source_target_pairs={{0,1},{1,0},{2,3},{3,2},{4,5},{5,4},{6,7},{7,6},{8,9},{9,8},{10,11... | collective-permute-start | bytes 983048 | tf_op jit(solution)/shard_map/ppermute | solution.py:31
  21.5 0.1 collective-permute-start.8
  21.6 0.0 collective-permute-done.6
  21.6 0.7 %broadcast_select_fusion = bf16[1,1,8,4,1280]{4,3,2,1,0:T(4,128)(2,1)} fusion(bf16[1,1,8,4,1280]{4,3,2,1,0:T(4,128)(2,1)S(1)} %collective-permute-done.6, pred[]{:T(512)S(6)} %eq.3), kind=kLoop, calls=%fused_computation | loop fusion | flops 40960 | bytes 163841 | tf_op jit(solution)/shard_map/jit(_where)/select_n | solution.py:305
  22.3 8.2 %collective-permute-done.8.other_ref = bf16[128,128]{1,0:T(8,128)(2,1)S(1)} collective-permute-done((bf16[128,128]{1,0:T(8,128)(2,1)S(1)}, bf16[128,128]{1,0:T(8,128)(2,1)S(1)}, u32[]{:S(2)}, u32[]{:S(2)}) %collective-permute-start.8) | collective-permute-done | bytes 32800 | tf_op jit(solution)/shard_map/ppermute | solution.py:31
  30.5 0.0 collective-permute-done.7.other_row_ref
  30.5 1.1 %shard_map.83 = f32[96,1280]{1,0:T(8,128)} custom-call(bf16[128,1280]{1,0:T(8,128)(2,1)S(1)} %shard_map.77.refs_0_.row_ref, bf16[128,128]{1,0:T(8,128)(2,1)S(1)} %get-tuple-element.20.mine_ref, bf16[128,1280]{1,0:T(8,128)(2,1)S(1)} %collective-permute-done.7.other_row_ref, bf16[128,128]{1,0:T(8,128)(2,1)S(1)} %collective-permute-done.8.other_ref), custom_call_target="tpu_custom_call" | custom-call | tf_op jit(solution)/shard_map/pallas_call | solution.py:306
  (6 shorter events, 0.0 us)
Async XLA Ops:
  0.6 5.8 %copy-start.3 = (bf16[1,1280,768]{2,1,0:T(8,128)(2,1)S(1)}, bf16[1,1280,768]{2,1,0:T(8,128)(2,1)}, u32[]{:S(2)}) copy-start(bf16[1,1280,768]{2,1,0:T(8,128)(2,1)} %param.11) | copy-start | bytes 5898244
  0.6 5.8 %copy-start.4 = (bf16[1,1,8,4,1280]{4,3,2,1,0:T(4,128)(2,1)S(1)}, bf16[1,1,8,4,1280]{4,3,2,1,0:T(4,128)(2,1)}, u32[]{:S(2)}) copy-start(bf16[1,1,8,4,1280]{4,3,2,1,0:T(4,128)(2,1)} %param.7) | copy-start | bytes 245764
  0.7 10.4 %collective-permute-start = (bf16[8,4,1280]{2,1,0:T(4,128)(2,1)}, bf16[8,4,1280]{2,1,0:T(4,128)(2,1)S(1)}, u32[]{:S(2)}, u32[]{:S(2)}) collective-permute-start(bf16[8,4,1280]{2,1,0:T(4,128)(2,1)} %bitcast.19), channel_id=1, source_target_pairs={{0,16},{8,24},{16,0},{24,8},{1,17},{9,25},{17,1},{25,9},{2,18},{10... | collective-permute-start | bytes 245768 | tf_op jit(solution)/shard_map/ppermute | solution.py:26
  4.8 7.7 %collective-permute-start.1 = (bf16[8,4,1280]{2,1,0:T(4,128)(2,1)}, bf16[8,4,1280]{2,1,0:T(4,128)(2,1)S(1)}, u32[]{:S(2)}, u32[]{:S(2)}) collective-permute-start(bf16[8,4,1280]{2,1,0:T(4,128)(2,1)} %bitcast.20), channel_id=1, source_target_pairs={{0,24},{8,16},{16,8},{24,0},{1,25},{9,17},{17,9},{25,1},{2,26},{10... | collective-permute-start | bytes 245768 | tf_op jit(solution)/shard_map/ppermute | solution.py:26
  6.1 6.4 %collective-permute-start.2 = (bf16[8,4,1280]{2,1,0:T(4,128)(2,1)}, bf16[8,4,1280]{2,1,0:T(4,128)(2,1)S(1)}, u32[]{:S(2)}, u32[]{:S(2)}) collective-permute-start(bf16[8,4,1280]{2,1,0:T(4,128)(2,1)} %bitcast.21), channel_id=1, source_target_pairs={{0,8},{8,0},{16,24},{24,16},{1,9},{9,1},{17,25},{25,17},{2,10},{10... | collective-permute-start | bytes 245768 | tf_op jit(solution)/shard_map/ppermute | solution.py:26
  6.4 6.2 %copy-start.1 = (bf16[1,1280,768]{2,1,0:T(8,128)(2,1)S(1)}, bf16[1,1280,768]{2,1,0:T(8,128)(2,1)}, u32[]{:S(2)}) copy-start(bf16[1,1280,768]{2,1,0:T(8,128)(2,1)} %param.9) | copy-start | bytes 5898244
  6.4 6.2 %copy-start.2 = (bf16[1,1280,768]{2,1,0:T(8,128)(2,1)S(1)}, bf16[1,1280,768]{2,1,0:T(8,128)(2,1)}, u32[]{:S(2)}) copy-start(bf16[1,1280,768]{2,1,0:T(8,128)(2,1)} %param.10) | copy-start | bytes 5898244
  6.4 6.1 %copy-start.5 = (bf16[1,1,8,4,1280]{4,3,2,1,0:T(4,128)(2,1)S(1)}, bf16[1,1,8,4,1280]{4,3,2,1,0:T(4,128)(2,1)}, u32[]{:S(2)}) copy-start(bf16[1,1,8,4,1280]{4,3,2,1,0:T(4,128)(2,1)} %param.6) | copy-start | bytes 245764
  6.4 6.2 %copy-start = (bf16[1,1280,768]{2,1,0:T(8,128)(2,1)S(1)}, bf16[1,1280,768]{2,1,0:T(8,128)(2,1)}, u32[]{:S(2)}) copy-start(bf16[1,1280,768]{2,1,0:T(8,128)(2,1)} %param.8) | copy-start | bytes 5898244
  6.9 9.4 %collective-permute-start.3 = (bf16[32,768]{1,0:T(8,128)(2,1)S(1)}, bf16[32,768]{1,0:T(8,128)(2,1)S(1)}, u32[]{:S(2)}, u32[]{:S(2)}) collective-permute-start(bf16[32,768]{1,0:T(8,128)(2,1)S(1)} %get-tuple-element.16.refs_1_), channel_id=1, source_target_pairs={{0,16},{8,24},{16,0},{24,8},{1,17},{9,25},{17,1},{25,9},{2,18},{10... | collective-permute-start | bytes 147464 | tf_op jit(solution)/shard_map/ppermute | solution.py:26
  9.7 6.6 %collective-permute-start.4 = (bf16[32,768]{1,0:T(8,128)(2,1)S(1)}, bf16[32,768]{1,0:T(8,128)(2,1)S(1)}, u32[]{:S(2)}, u32[]{:S(2)}) collective-permute-start(bf16[32,768]{1,0:T(8,128)(2,1)S(1)} %get-tuple-element.16.refs_1_), channel_id=1, source_target_pairs={{0,24},{8,16},{16,8},{24,0},{1,25},{9,17},{17,9},{25,1},{2,26},{10... | collective-permute-start | bytes 147464 | tf_op jit(solution)/shard_map/ppermute | solution.py:26
  11.1 5.3 %collective-permute-start.5 = (bf16[32,768]{1,0:T(8,128)(2,1)S(1)}, bf16[32,768]{1,0:T(8,128)(2,1)S(1)}, u32[]{:S(2)}, u32[]{:S(2)}) collective-permute-start(bf16[32,768]{1,0:T(8,128)(2,1)S(1)} %get-tuple-element.16.refs_1_), channel_id=1, source_target_pairs={{0,8},{8,0},{16,24},{24,16},{1,9},{9,1},{17,25},{25,17},{2,10},{10... | collective-permute-start | bytes 147464 | tf_op jit(solution)/shard_map/ppermute | solution.py:26
  19.4 2.2 %collective-permute-start.6 = (bf16[1,1,8,4,1280]{4,3,2,1,0:T(4,128)(2,1)S(1)}, bf16[1,1,8,4,1280]{4,3,2,1,0:T(4,128)(2,1)S(1)}, u32[]{:S(2)}, u32[]{:S(2)}) collective-permute-start(bf16[1,1,8,4,1280]{4,3,2,1,0:T(4,128)(2,1)S(1)} %bitcast.17), channel_id=1, source_target_pairs={{0,6},{2,0},{4,2},{6,4},{1,7},{3,1},{5,3},{7,5},{8,14},{10,8},{12,... | collective-permute-start | bytes 245768 | tf_op jit(solution)/shard_map/ppermute | solution.py:31
  19.5 11.0 %collective-permute-start.7 = (bf16[128,1280]{1,0:T(8,128)(2,1)S(1)}, bf16[128,1280]{1,0:T(8,128)(2,1)S(1)}, u32[]{:S(2)}, u32[]{:S(2)}) collective-permute-start(bf16[128,1280]{1,0:T(8,128)(2,1)S(1)} %shard_map.77.refs_0_.row_ref), channel_id=1, source_target_pairs={{0,1},{1,0},{2,3},{3,2},{4,5},{5,4},{6,7},{7,6},{8,9},{9,8},{10,11... | collective-permute-start | bytes 983048 | tf_op jit(solution)/shard_map/ppermute | solution.py:31
  21.5 9.0 %collective-permute-start.8 = (bf16[128,128]{1,0:T(8,128)(2,1)S(1)}, bf16[128,128]{1,0:T(8,128)(2,1)S(1)}, u32[]{:S(2)}, u32[]{:S(2)}) collective-permute-start(bf16[128,128]{1,0:T(8,128)(2,1)S(1)} %get-tuple-element.21), channel_id=1, source_target_pairs={{0,1},{1,0},{2,3},{3,2},{4,5},{5,4},{6,7},{7,6},{8,9},{9,8},{10,11... | collective-permute-start | bytes 98312 | tf_op jit(solution)/shard_map/ppermute | solution.py:31
